TPU v7x, 512 devices: a whole 4x8x8 slice. The times are simulated.
512 devices in a mesh: sec: 64 (over y, z), term: 8 (over x, core).
Axes of the slice: x: 4, y: 8, z: 8, core: 2. Of those that a mesh axis runs over, the one named last changes fastest.
Arguments:
- psi: bfloat16 [64, 3, 256, 256], P('sec'), may hold values from -6 to 6
- left_ops: bfloat16 [64, 64, 256, 256], P('term', 'sec'), may hold values from -0.375 to 0.375
- right_ops: bfloat16 [64, 64, 256, 256], P('term', 'sec'), may hold values from -0.046875 to 0.046875
- left_dims: int32 [64], replicated, may hold values from 1 to 256, 8192 in all
- right_dims: int32 [64], replicated, may hold values from 1 to 256, 8192 in all
Outputs:
- new_state: bfloat16 [64, 3, 256, 256], P('sec')
- kept: float32 [64, 256, 256], P('sec')
- energy: float32 [], replicated
Inputs may be any that keep to these rules, and one draw needn't show every extreme that they name: `left_dims`: the 64 sector dimensions sum to 8192 and the largest is exactly 256. `right_dims`: the 64 sector dimensions sum to 8192 and the largest is exactly 256.
All inputs are finite; a program needn't handle non-finite values.
Results may differ from a plain program's by a relative error of at most 0.0058.
Values may be sent and summed in bfloat16 or wider, within the bound.
A program may use at most 64 MiB of HBM per device.

v0:
```python
import jax
import jax.numpy as jnp
from jax import lax
from jax.sharding import PartitionSpec as P

SIGN_STEPS = 6


noise_weight = 0.5
highest = lax.Precision.HIGHEST


def passed_along(value, axis, by):
    length = lax.axis_size(axis)
    pairs = [(i, i + by) for i in range(length) if 0 <= i + by < length]
    return lax.ppermute(value, axis, pairs)


def symmetric(blocks):
    widened = blocks.astype(jnp.float32)
    return (widened + jnp.swapaxes(widened, -1, -2)).astype(jnp.bfloat16)


def subspace(a11, h11, a12, a22, h12, h22):
    quad_a = a11 * a22 - a12 * a12
    quad_b = h11 * a22 + h22 * a11 - 2.0 * h12 * a12
    quad_c = h11 * h22 - h12 * h12
    lowest = (quad_b - jnp.sqrt(jnp.maximum(quad_b * quad_b - 4.0 * quad_a * quad_c, 0.0))) / (
        2.0 * quad_a
    )
    ratio = (lowest * a11 - h11) / (h12 - lowest * a12)
    scale = lax.rsqrt(a11 + 2.0 * ratio * a12 + ratio * ratio * a22)
    return (lowest, scale, ratio * scale)


def sign_projector(density, live_count):
    order_size = density.shape[-1]
    identity = jnp.eye(order_size, dtype=jnp.float32)
    mean_value = jnp.trace(density, axis1=-2, axis2=-1) / live_count
    shifted = density - mean_value[:, None, None] * identity
    frobenius = jnp.sqrt(jnp.sum(shifted * shifted, axis=(1, 2), keepdims=True))
    current = shifted / frobenius
    for repeat in range(SIGN_STEPS):
        squared = jnp.matmul(current, current, precision=highest)
        cubed_term = jnp.matmul(squared, current, precision=highest)
        current = 1.5 * current - 0.5 * cubed_term
    return 0.5 * (identity + current)


def apply_terms(sym_left, sym_right, blocks, mask):
    images = jnp.einsum(
        "tkij,kjl->tkil", sym_left, blocks, preferred_element_type=jnp.float32
    ).astype(jnp.bfloat16)
    term_part = (
        jnp.einsum("tkil,tlm->kim", images, sym_right, preferred_element_type=jnp.float32) * mask
    )
    return (images, term_part)


def reduce_whole(term_part):
    return lax.psum(term_part, "term")


def sums_sector(values):
    return lax.psum(values, "sec")


def per_device(psi, left_ops, right_ops, left_dims, right_dims):
    span = psi.shape[1]
    width = psi.shape[2]
    sector_count = left_dims.shape[0]
    total_terms = left_ops.shape[0] * lax.axis_size("term")
    own_sector = lax.axis_index("sec")
    states = jnp.arange(width, dtype=jnp.int32)
    sectors = jnp.arange(sector_count, dtype=jnp.int32)
    paired = own_sector + jnp.arange(span, dtype=jnp.int32)
    select = paired[:, None] == sectors[None, :]
    pair_dims = jnp.sum(jnp.where(select, left_dims[None, :], 0), axis=1)
    own_select = sectors == own_sector
    own_left = jnp.sum(jnp.where(own_select, left_dims, 0))
    own_right = jnp.sum(jnp.where(own_select, right_dims, 0))
    left_live = (states[None, :] < pair_dims[:, None]).astype(jnp.float32)
    right_live = (states < own_right).astype(jnp.float32)
    mask = left_live[:, :, None] * right_live[None, None, :]
    left_parts = [left_ops]
    for offset in range(1, span):
        left_parts.append(passed_along(left_ops, "sec", -offset))
    sym_left = symmetric(jnp.concatenate(left_parts, axis=1))
    sym_right = symmetric(right_ops[:, 0])
    vector = psi[0] * mask.astype(jnp.bfloat16)
    images_first, term_first = apply_terms(sym_left, sym_right, vector, mask)
    vector_wide = vector.astype(jnp.float32)
    sigma_first = reduce_whole(term_first)
    a11, h11 = sums_sector((jnp.sum(vector_wide * vector_wide), jnp.sum(vector_wide * sigma_first)))
    correction = (sigma_first - h11 / a11 * vector_wide).astype(jnp.bfloat16)
    images_second, term_second = apply_terms(sym_left, sym_right, correction, mask)
    sigma_second = reduce_whole(term_second)
    corr_wide = correction.astype(jnp.float32)
    a12, a22, h12, h22 = sums_sector(
        (
            jnp.sum(vector_wide * corr_wide),
            jnp.sum(corr_wide * corr_wide),
            jnp.sum(vector_wide * sigma_second),
            jnp.sum(corr_wide * sigma_second),
        )
    )
    energy, first_coef, second_coef = subspace(a11, h11, a12, a22, h12, h22)
    new_state = (first_coef * vector_wide + second_coef * corr_wide).astype(jnp.bfloat16)
    weighted = (
        (
            first_coef * images_first.astype(jnp.float32)
            + second_coef * images_second.astype(jnp.float32)
        )
        * left_live[None, :, :, None]
    ).astype(jnp.bfloat16)
    noise_local = jnp.einsum(
        "tkil,tkjl->kij", weighted, weighted, preferred_element_type=jnp.float32
    )
    noise_total = lax.psum(noise_local.astype(jnp.bfloat16), "term").astype(jnp.float32)
    own_part = jnp.einsum("kil,kjl->kij", new_state, new_state, preferred_element_type=jnp.float32)
    pieces = own_part + noise_weight / total_terms * noise_total
    density = pieces[0]
    for offset in range(1, span):
        density = density + passed_along(pieces[offset], "sec", offset)
    kept = sign_projector(density[None], own_left.astype(jnp.float32)[None])
    return (new_state[None], kept, energy)


def solution(mesh):
    in_specs = (
        P("sec", None, None, None),
        P("term", "sec", None, None),
        P("term", "sec", None, None),
        P(),
        P(),
    )
    out_specs = (P("sec", None, None, None), P("sec", None, None), P())
    return jax.shard_map(
        per_device, mesh=mesh, in_specs=in_specs, out_specs=out_specs, check_vma=False
    )
```

profile of v0, /device:TPU:1, one launch (start us, length us, event | category | flops | bytes accessed | tf_op | source)
XLA Modules:
  0.0 659.2 jit_solution(13804254643983725885)
XLA Ops:
  7.2 1.3 collective-permute-start.1
  8.5 1.3 collective-permute-start
  9.8 1.5 bitcast_convert_fusion
  11.4 1.9 copy.21
  13.2 0.6 fusion.65
  13.9 0.6 compare_convert_fusion
  14.5 0.2 select_reduce_fusion.1
  14.7 0.1 fusion.64
  14.8 46.6 %collective-permute-done.1 = bf16[8,1,256,256]{3,2,1,0:T(8,128)(2,1)} collective-permute-done((bf16[8,1,256,256]{3,2,1,0:T(8,128)(2,1)}, bf16[8,1,256,256]{3,2,1,0:T(8,128)(2,1)}, u32[]{:S(2)}, u32[]{:S(2)}) %collective-permute-start.1) | collective-permute-done | bytes 1048608 | tf_op jit(solution)/shard_map/ppermute | solution.py:16
  61.4 17.2 %collective-permute-done = bf16[8,1,256,256]{3,2,1,0:T(8,128)(2,1)} collective-permute-done((bf16[8,1,256,256]{3,2,1,0:T(8,128)(2,1)}, bf16[8,1,256,256]{3,2,1,0:T(8,128)(2,1)}, u32[]{:S(2)}, u32[]{:S(2)}) %collective-permute-start) | collective-permute-done | bytes 1048608 | tf_op jit(solution)/shard_map/ppermute | solution.py:16
  78.6 4.6 maximum_convert_fusion
  83.2 6.6 %copy.18 = f32[8,3,256,256]{2,3,1,0:T(8,128)} copy(f32[8,3,256,256]{3,2,1,0:T(8,128)} %maximum_convert_fusion) | data formatting | bytes 12582912 | tf_op jit(solution)/shard_map/convert_element_type | solution.py:20
  89.8 4.2 fusion
  94.0 1.3 fusion.15
  95.3 1.7 copy-done.4
  97.0 1.9 multiply_multiply_fusion.1
  98.9 79.4 %all-reduce.6.cloned.1.call-done = f32[3,256,256]{2,1,0:T(8,128)} async-done(((f32[3,256,256]{2,1,0:T(8,128)}), f32[3,256,256]{2,1,0:T(8,128)}) %all-reduce.6.cloned.1.call-update) | async-done | bytes 786448 | tf_op jit(solution)/shard_map/psum | solution.py:61
  178.4 2.0 fusion.47
  180.4 116.7 %all-reduce.1 = (f32[]{:T(128)}, f32[]{:T(128)}) all-reduce(f32[]{:T(128)} %get-tuple-element.7, f32[]{:T(128)} %get-tuple-element.6), channel_id=1, replica_groups=mesh['sec'=64,'term'=8] {'sec'}, use_global_device_ids=true, to_apply=%region_6.7 | all-reduce | flops 2 | bytes 16 | tf_op jit(solution)/shard_map/psum | solution.py:65
  298.5 1.3 fusion.50
  299.9 1.0 fusion.18
  300.9 1.7 copy-done.5
  302.6 1.9 multiply_multiply_fusion
  304.6 91.8 %all-reduce.8.cloned.1.call-done = f32[3,256,256]{2,1,0:T(8,128)} async-done(((f32[3,256,256]{2,1,0:T(8,128)}), f32[3,256,256]{2,1,0:T(8,128)}) %all-reduce.8.cloned.1.call-update) | async-done | bytes 786448 | tf_op jit(solution)/shard_map/psum | solution.py:61
  396.4 2.3 fusion.51
  398.7 116.9 %all-reduce = (f32[]{:T(128)}, f32[]{:T(128)}, f32[]{:T(128)}, f32[]{:T(128)}) all-reduce(f32[]{:T(128)} %get-tuple-element.8, f32[]{:T(128)} %get-tuple-element.4, f32[]{:T(128)} %get-tuple-element.3, f32[]{:T(128)} %get-tuple-element.5), channel_id=1, replica_groups=mesh['sec'=64,'term'=8] {'sec'}, use_global_device_ids=true, to_apply=%region_8.9 | all-reduce | flops 4 | bytes 32 | tf_op jit(solution)/shard_map/psum | solution.py:65
  529.5 8.5 %fusion.33 = bf16[3,256,256]{2,1,0:T(8,128)(2,1)} fusion(bf16[3,256,8,256]{3,1,2,0:T(8,128)(2,1)} %copy-done.5, bf16[3,256,8,256]{3,1,2,0:T(8,128)(2,1)} %copy-done.4, f32[3,256]{1,0:T(4,128)S(1)} %fusion.64, f32[]{:T(128)S(6)} %mul.238, f32[]{:T(128)S(6)} %rsqrt.3), kind=kOutput, calls=%fused_computation.38 | convolution fusion | flops 816513024 | bytes 6687752 | tf_op jit(solution)/shard_map/tkil,tkjl->kij/dot_general | solution.py:116
  538.0 90.8 %all-reduce.10.cloned.1.call-done = bf16[3,256,256]{2,1,0:T(8,128)(2,1)} async-done(((bf16[3,256,256]{2,1,0:T(8,128)(2,1)}), bf16[3,256,256]{2,1,0:T(8,128)(2,1)}) %all-reduce.10.cloned.1.call-update) | async-done | bytes 393232 | tf_op jit(solution)/shard_map/psum | solution.py:119
  628.8 1.5 convolution_add_fusion
  630.4 3.7 collective-permute-start.3
  634.1 3.3 collective-permute-start.2
  637.4 0.6 fusion.66
  638.7 1.0 fusion.63
  639.7 3.8 collective-permute-done.2
  643.5 0.7 select_reduce_fusion
  644.8 0.7 multiply_reduce_fusion
  646.1 0.4 fusion.59
  646.6 0.4 multiply_subtract_fusion
  647.0 0.4 fusion.74
  647.4 0.4 fusion.38
  647.8 0.4 fusion.75
  648.1 0.4 fusion.37
  648.5 0.4 fusion.76
  648.9 0.4 fusion.36
  649.3 0.4 fusion.77
  649.7 0.4 fusion.35
  650.1 0.4 fusion.78
  650.5 1.1 fusion.41
  (31 shorter events, 0.3 us)
Async XLA Ops:
  7.2 171.2 %all-reduce.6.cloned.1.call-start = ((), (), s32[]{:S(2)}) async-start(), calls=%async_computation | async-start | bytes 1572864 | tf_op jit(solution)/shard_map/psum | solution.py:61
  7.2 54.1 %collective-permute-start.1 = (bf16[8,1,256,256]{3,2,1,0:T(8,128)(2,1)}, bf16[8,1,256,256]{3,2,1,0:T(8,128)(2,1)}, u32[]{:S(2)}, u32[]{:S(2)}) collective-permute-start(bf16[8,1,256,256]{3,2,1,0:T(8,128)(2,1)} %param.6), channel_id=1, source_target_pairs={{16,0},{24,8},{32,16},{40,24},{48,32},{56,40},{64,48},{72,56},{80,... | collective-permute-start | bytes 3145736 | tf_op jit(solution)/shard_map/ppermute | solution.py:16
  8.5 70.1 %collective-permute-start = (bf16[8,1,256,256]{3,2,1,0:T(8,128)(2,1)}, bf16[8,1,256,256]{3,2,1,0:T(8,128)(2,1)}, u32[]{:S(2)}, u32[]{:S(2)}) collective-permute-start(bf16[8,1,256,256]{3,2,1,0:T(8,128)(2,1)} %param.6), channel_id=1, source_target_pairs={{8,0},{16,8},{24,16},{32,24},{40,32},{48,40},{56,48},{64,56},{72,6... | collective-permute-start | bytes 3145736 | tf_op jit(solution)/shard_map/ppermute | solution.py:16
  9.8 3.4 copy-start.10
  9.8 4.7 copy-start.11
  9.8 68.7 %copy-start.3 = (bf16[8,1,256,256]{3,2,1,0:T(8,128)(2,1)S(1)}, bf16[8,1,256,256]{3,2,1,0:T(8,128)(2,1)}, u32[]{:S(2)}) copy-start(bf16[8,1,256,256]{3,2,1,0:T(8,128)(2,1)} %param.6) | copy-start | bytes 3145732
  89.8 4.2 copy-start
  94.0 3.0 copy-start.6
  94.0 3.0 copy-start.8
  95.3 1.7 copy-start.4
  98.9 297.5 %all-reduce.8.cloned.1.call-start = ((), (), s32[]{:S(2)}) async-start(), calls=%async_computation.1 | async-start | bytes 1572864 | tf_op jit(solution)/shard_map/psum | solution.py:61
  299.8 1.1 copy-start.1
  299.8 2.8 copy-start.7
  299.9 2.8 copy-start.9
  300.9 1.7 copy-start.5
  304.5 324.3 %all-reduce.10.cloned.1.call-start = ((), (), s32[]{:S(2)}) async-start(), calls=%async_computation.2 | async-start | bytes 786432 | tf_op jit(solution)/shard_map/psum | solution.py:119
  529.5 99.3 %copy-start.2 = (bf16[3,256,256]{2,1,0:T(8,128)(2,1)S(1)}, bf16[3,256,256]{2,1,0:T(8,128)(2,1)}, u32[]{:S(2)}) copy-start(bf16[3,256,256]{2,1,0:T(8,128)(2,1)} %copy-done.1) | copy-start | bytes 1179652
  630.4 9.2 %collective-permute-start.3 = (f32[256,256]{1,0:T(8,128)S(1)}, f32[256,256]{1,0:T(8,128)S(1)}, u32[]{:S(2)}, u32[]{:S(2)}) collective-permute-start(f32[256,256]{1,0:T(8,128)S(1)} %get-tuple-element.18), channel_id=1, source_target_pairs={{0,16},{8,24},{16,32},{24,40},{32,48},{40,56},{48,64},{56,72},{64,... | collective-permute-start | bytes 786440 | tf_op jit(solution)/shard_map/ppermute | solution.py:16
  634.1 9.4 %collective-permute-start.2 = (f32[256,256]{1,0:T(8,128)S(1)}, f32[256,256]{1,0:T(8,128)S(1)}, u32[]{:S(2)}, u32[]{:S(2)}) collective-permute-start(f32[256,256]{1,0:T(8,128)S(1)} %get-tuple-element.17), channel_id=1, source_target_pairs={{0,8},{8,16},{16,24},{24,32},{32,40},{40,48},{48,56},{56,64},{64,7... | collective-permute-start | bytes 786440 | tf_op jit(solution)/shard_map/ppermute | solution.py:16
Sparse Core Ops, SparseCore 0:
  99.0 79.3 all-reduce.5
  304.7 91.7 all-reduce.7
  538.2 90.6 all-reduce.9
where the time goes:
time: 671 us; the launch traced here: 659 us
  waiting for transfers between devices  330 us (49%)
  blocking collectives  234 us (35%)
  between operations  32.3 us (5%)
  matrix products  21.5 us (3%)
  other arithmetic  20.5 us (3%)
  local copies, waits for them, and re-layouts  11.9 us (2%)
  starting transfers between devices  9.64 us (1%)
    psum x2, blocking collectives, sums_sector(): return lax.psum(values, 'sec')  234 us
    psum x2, waiting for transfers between devices, reduce_whole(): return lax.psum(term_part, 'term')  171 us
    psum x1, waiting for transfers between devices, per_device(): lax.psum(noise_local.astype(jnp.bfloat16), 'term').astype(jnp.float32)  90.8 us
    ppermute x4, waiting for transfers between devices, passed_along(): return lax.ppermute(value, axis, pairs)  67.6 us
  transfers between devices with their start and end apart: 7, of which 6 were waited for; matrix products, arithmetic and copies ran while one was open for 1% of the time, Pallas kernels for 0%

commit v1 on v0

v1 whole, which is shorter than its diff:
```python
import functools

import jax
import jax.numpy as jnp
from jax import lax
from jax.experimental import pallas as pl
from jax.experimental.pallas import tpu as pltpu
from jax.sharding import PartitionSpec as P

SIGN_STEPS = 6
ZSIZE = 8
CORES = 2
NOISE_WEIGHT = 0.5
MESH = pl.DeviceIdType.MESH
F32 = jnp.float32
BF16 = jnp.bfloat16


def dot(a, b):
    return jnp.dot(a, b, preferred_element_type=F32)


def dot_t(a, b):
    return lax.dot_general(a, b, (((1,), (1,)), ((), ())), preferred_element_type=F32)


def fold(value):
    half = value.shape[1] // 2
    row = jnp.sum(value, axis=0, keepdims=True)
    return row[:, :half] + row[:, half:]


def kernel(
    sizes,
    left_dims, right_dims, psi, left, right,
    new_state, kept, energy,
    sl0, sr0, sl1, sr1, pack_l, pack_r, got_l, got_r, got_psi,
    vec, cor, img_a, img_b, acc, nacc, half_a, half_n, core_a, core_n, part_a, part_n,
    sums, totals, ns_mine, ns_got, piece_out, piece_in, dens,
    pack_send, pack_recv, one_send, one_recv, x_send, x_recv, s_send, s_recv,
):
    ns, zs, tg, terms, width = sizes
    ys, xs = ns // zs, tg // CORES
    half, quarter = width // 2, width // 2 // xs
    me, lane = lax.axis_index("sec"), lax.axis_index("term")
    x, c = lax.div(lane, CORES), lax.rem(lane, CORES)
    y, z = lax.div(me, zs), lax.rem(me, zs)
    up, down = lax.rem(me + 1, ns), lax.rem(me + ns - 1, ns)
    partner = lane + 1 - 2 * c
    lanes_x = [lax.rem(x + d, xs) * CORES + c for d in range(1, xs)]
    in_x = [lax.rem(x + d, xs) for d in range(1, xs)]

    def send(src, dst, ssem, rsem, sec, term):
        return pltpu.make_async_remote_copy(
            src_ref=src, dst_ref=dst, send_sem=ssem, recv_sem=rsem,
            device_id=(sec, term), device_id_type=MESH,
        )

    barrier = pltpu.get_barrier_semaphore()
    groups = [
        [((me, lax.rem(lane + d, tg)), lax.rem(lane + d, tg)) for d in range(1, tg)],
        [((y * zs + lax.rem(z + d, zs), lane), lax.rem(z + d, zs)) for d in range(1, zs)],
        [((lax.rem(y + d, ys) * zs + z, lane), lax.rem(y + d, ys)) for d in range(1, ys)],
    ]
    places = [lane, z, y]
    greeted = [peer for group in groups for peer, _ in group] + [(up, lane), (down, lane)]
    for peer in greeted:
        pl.semaphore_signal(barrier, inc=1, device_id=peer, device_id_type=MESH)

    row_h = lax.broadcasted_iota(jnp.int32, (half, half), 0)
    col_h = lax.broadcasted_iota(jnp.int32, (half, half), 1)

    def prepare(t, raw, sym, pack):
        wide = raw[t].astype(F32)
        whole = (wide + wide.T).astype(BF16)
        sym[t] = whole
        again = whole.astype(F32)
        low, high = again[:half, :half], again[half:, half:]
        pack[t, :half] = whole[:half, half:]
        pack[t, half:width] = jnp.where(row_h <= col_h, low, high).astype(BF16)
        diag = jnp.sum(jnp.where(row_h == col_h, high, 0.0), axis=0, keepdims=True)
        pack[t, width:] = jnp.broadcast_to(diag, (16, half)).astype(BF16)

    def restore(t, pack, sym):
        corner = pack[t, :half].astype(F32)
        mixed = pack[t, half:width].astype(F32)
        diag = pack[t, width:].astype(F32)[0:1]
        turned = mixed.T
        sym[t, :half, :half] = jnp.where(row_h <= col_h, mixed, turned).astype(BF16)
        sym[t, :half, half:] = pack[t, :half]
        sym[t, half:, :half] = corner.T.astype(BF16)
        lower = jnp.where(row_h == col_h, jnp.broadcast_to(diag, (half, half)), turned)
        sym[t, half:, half:] = jnp.where(row_h > col_h, mixed, lower).astype(BF16)

    def ops_copies(t):
        return (
            send(pack_l.at[t], got_l.at[t], pack_send.at[0, t], pack_recv.at[0, t], down, lane),
            send(pack_r.at[t], got_r.at[t], pack_send.at[1, t], pack_recv.at[1, t], up, lane),
        )

    prepare(0, left, sl0, pack_l)
    prepare(0, right, sr0, pack_r)
    pl.semaphore_wait(barrier, len(greeted))
    psi_copy = send(psi.at[2], got_psi, one_send.at[0], one_recv.at[0], up, lane)
    psi_copy.start()

    @pl.loop(1, terms)
    def _(t):
        prepare(t, left, sl0, pack_l)
        prepare(t, right, sr0, pack_r)
        for copy in ops_copies(t - 1):
            copy.start()

    inside = me + 1 < ns
    rows_own = left_dims[me]
    rows_next = jnp.where(inside, left_dims[up], 0)
    cols_own = right_dims[me]
    cols_last = jnp.where(me >= 1, right_dims[down], 0)
    live_rows = [rows_own, rows_next, rows_next]
    live_cols = [cols_own, cols_own, cols_last]

    def mask_of(k, first_row, count):
        row = lax.broadcasted_iota(jnp.int32, (count, width), 0) + first_row
        col = lax.broadcasted_iota(jnp.int32, (count, width), 1)
        return (row < live_rows[k]) & (col < live_cols[k])

    for k in range(2):
        vec[k] = jnp.where(mask_of(k, 0, width), psi[k].astype(F32), 0.0).astype(BF16)
    for copy in ops_copies(terms - 1):
        copy.start()

    def part_own(t, blocks, images):
        image = dot(sl0[t], blocks[0]).astype(BF16)
        images[t, 0] = image
        acc[0] += dot(image, sr0[t])

    def part_near(t, blocks, images):
        one = dot(sl1[t], blocks[1]).astype(BF16)
        two = dot(sl1[t], blocks[2]).astype(BF16)
        images[t, 1] = one
        images[t, 2] = two
        acc[1] += dot(one, sr0[t])
        acc[2] += dot(two, sr1[t])

    acc[...] = jnp.zeros_like(acc)

    @pl.loop(0, terms)
    def _(t):
        part_own(t, vec, img_a)

    psi_copy.wait_recv()
    vec[2] = jnp.where(mask_of(2, 0, width), got_psi[...].astype(F32), 0.0).astype(BF16)

    @pl.loop(0, terms)
    def _(t):
        for copy in ops_copies(t):
            copy.wait_recv()
        restore(t, got_l, sl1)
        restore(t, got_r, sr1)
        part_near(t, vec, img_a)

    def scalar_round(rnd, stage):
        copies = []
        for d, (peer, _) in enumerate(groups[stage]):
            copies.append(send(
                sums.at[rnd, stage, places[stage]], sums.at[rnd, stage, places[stage]],
                s_send.at[rnd, stage, d], s_recv.at[rnd, stage, places[stage]], *peer,
            ))
        return copies

    def scalar_wait(rnd, stage, copies):
        for d, (peer, place) in enumerate(groups[stage]):
            send(
                sums.at[rnd, stage, place], sums.at[rnd, stage, place],
                s_send.at[rnd, stage, d], s_recv.at[rnd, stage, place], *peer,
            ).wait_recv()
        total = sums[rnd, stage, 0]
        for i in range(1, len(groups[stage]) + 1):
            total = total + sums[rnd, stage, i]
        return total

    waits = []

    def start_all(copies):
        for copy in copies:
            copy.start()
        waits.extend(copies)

    def put_rows(rnd, rows):
        rows = rows + [jnp.zeros((8 - len(rows), half), F32)]
        sums[rnd, 0, lane] = jnp.concatenate(rows, axis=0)

    mine = pl.multiple_of(c * half, half)
    other = pl.multiple_of((1 - c) * half, half)
    own_row = pl.multiple_of(c * half + x * quarter, quarter)
    share = pl.ds(pl.multiple_of(x * quarter, quarter), quarter)

    def x_scatter(src, dst, base):
        return [
            send(
                src.at[:, pl.ds(pl.multiple_of(in_x[i] * quarter, quarter), quarter), :],
                dst.at[x], x_send.at[base, i], x_recv.at[base, x], me, lanes_x[i],
            )
            for i in range(xs - 1)
        ]

    def x_wait(src, dst, base):
        for i in range(xs - 1):
            send(
                src.at[:, share, :], dst.at[in_x[i]],
                x_send.at[base, i], x_recv.at[base, in_x[i]], me, lanes_x[i],
            ).wait_recv()

    def rows_at(ref, index):
        start = pl.multiple_of(c * half + index * quarter, quarter)
        return ref.at[..., pl.ds(start, quarter), :]

    def x_gather(ref, base):
        return [
            send(
                rows_at(ref, x), rows_at(ref, x), x_send.at[base, i], x_recv.at[base, x],
                me, lanes_x[i],
            )
            for i in range(xs - 1)
        ]

    def x_gather_wait(ref, base):
        for i in range(xs - 1):
            send(
                rows_at(ref, in_x[i]), rows_at(ref, in_x[i]), x_send.at[base, i],
                x_recv.at[base, in_x[i]], me, lanes_x[i],
            ).wait_recv()

    def core_gather(ref, slot):
        piece = ref.at[..., pl.ds(mine, half), :]
        return send(piece, piece, one_send.at[slot], one_recv.at[slot], me, partner)

    def core_gather_wait(ref, slot):
        piece = ref.at[..., pl.ds(other, half), :]
        send(piece, piece, one_send.at[slot], one_recv.at[slot], me, partner).wait_recv()

    h11 = a11 = jnp.zeros((1, half), F32)
    for k in range(3):
        wide = vec[k].astype(F32)
        h11 = h11 + fold(wide * acc[k])
        a11 = a11 + fold(wide * wide)
    put_rows(0, [h11, a11])
    core_copy = send(
        acc.at[:, pl.ds(other, half), :], core_a, one_send.at[1], one_recv.at[1], me, partner
    )
    start_all([core_copy])
    start_all(scalar_round(0, 0))
    core_copy.wait_recv()
    half_a[...] = acc[:, pl.ds(mine, half), :] + core_a[...]
    sums[0, 1, z] = scalar_wait(0, 0, None)
    start_all(x_scatter(half_a, part_a, 0))
    start_all(scalar_round(0, 1))
    sums[0, 2, y] = scalar_wait(0, 1, None)
    x_wait(half_a, part_a, 0)
    part_a[x] = half_a[:, share, :]
    start_all(scalar_round(0, 2))
    shard = part_a[0]
    for i in range(1, xs):
        shard = shard + part_a[i]
    total = scalar_wait(0, 2, None)
    h11 = jnp.sum(total[0:1], axis=1, keepdims=True)
    a11 = jnp.sum(total[1:2], axis=1, keepdims=True) * (1.0 / tg)
    level = h11 / a11
    for k in range(3):
        held = vec[k, pl.ds(own_row, quarter), :].astype(F32)
        inside_k = jnp.where(mask_of(k, own_row, quarter), shard[k], 0.0)
        cor[k, pl.ds(own_row, quarter), :] = (inside_k - level * held).astype(BF16)
    start_all(x_gather(cor, 1))
    x_gather_wait(cor, 1)
    core_copy_two = core_gather(cor, 2)
    start_all([core_copy_two])
    core_copy.wait_send()
    acc[...] = jnp.zeros_like(acc)
    core_gather_wait(cor, 2)

    @pl.loop(0, terms)
    def _(t):
        part_own(t, cor, img_b)
        part_near(t, cor, img_b)

    a12 = a22 = h12 = h22 = jnp.zeros((1, half), F32)
    for k in range(3):
        wide, corr = vec[k].astype(F32), cor[k].astype(F32)
        summed = acc[k]
        a12 = a12 + fold(wide * corr)
        a22 = a22 + fold(corr * corr)
        h12 = h12 + fold(wide * summed)
        h22 = h22 + fold(corr * summed)
    put_rows(1, [a12, a22, h12, h22])
    start_all(scalar_round(1, 0))
    sums[1, 1, z] = scalar_wait(1, 0, None)
    start_all(scalar_round(1, 1))
    sums[1, 2, y] = scalar_wait(1, 1, None)
    start_all(scalar_round(1, 2))
    total = scalar_wait(1, 2, None)
    whole = jnp.sum(total, axis=1, keepdims=True)
    a12, a22 = whole[0:1] * (1.0 / tg), whole[1:2] * (1.0 / tg)
    h12, h22 = whole[2:3], whole[3:4]
    quad_a = a11 * a22 - a12 * a12
    quad_b = h11 * a22 + h22 * a11 - 2.0 * h12 * a12
    quad_c = h11 * h22 - h12 * h12
    lowest = (quad_b - jnp.sqrt(jnp.maximum(quad_b * quad_b - 4.0 * quad_a * quad_c, 0.0))) / (
        2.0 * quad_a
    )
    ratio = (lowest * a11 - h11) / (h12 - lowest * a12)
    first_coef = lax.rsqrt(a11 + 2.0 * ratio * a12 + ratio * ratio * a22)
    second_coef = ratio * first_coef
    energy[...] = lowest

    for k in range(3):
        ns_mine[k] = (first_coef * vec[k].astype(F32) + second_coef * cor[k].astype(F32)).astype(BF16)
    nacc[...] = jnp.zeros_like(nacc)

    @pl.loop(0, terms)
    def _(t):
        for k in range(3):
            row = lax.broadcasted_iota(jnp.int32, (width, width), 0)
            mixed = first_coef * img_a[t, k].astype(F32) + second_coef * img_b[t, k].astype(F32)
            weighted = jnp.where(row < live_rows[k], mixed, 0.0).astype(BF16)
            nacc[min(k, 1)] += dot_t(weighted, weighted)

    ns_copy = send(ns_mine.at[2], ns_got, one_send.at[3], one_recv.at[3], down, lane)
    core_noise = send(
        nacc.at[:, pl.ds(other, half), :], core_n, one_send.at[4], one_recv.at[4], me, partner
    )
    new_state[0] = ns_mine[0]
    new_state[1] = ns_mine[1]
    start_all([core_noise])
    own = [dot_t(ns_mine[k, pl.ds(own_row, quarter), :], ns_mine[k]) for k in range(3)]
    core_noise.wait_recv()
    half_n[...] = nacc[:, pl.ds(mine, half), :] + core_n[...]
    start_all([ns_copy])
    start_all(x_scatter(half_n, part_n, 2))
    x_wait(half_n, part_n, 2)
    part_n[x] = half_n[:, share, :]
    noise = part_n[0]
    for i in range(1, xs):
        noise = noise + part_n[i]
    scale = NOISE_WEIGHT / (terms * tg)
    piece_out[...] = own[1] + own[2] + scale * noise[1]
    piece_copy = send(piece_out, piece_in, one_send.at[5], one_recv.at[5], up, lane)
    start_all([piece_copy])
    stay = own[0] + scale * noise[0]
    piece_copy.wait_recv()
    dens[pl.ds(own_row, quarter), :] = stay + piece_in[...]
    start_all(x_gather(dens, 3))
    x_gather_wait(dens, 3)
    dens_copy = core_gather(dens, 6)
    start_all([dens_copy])
    ns_copy.wait_recv()
    new_state[2] = ns_got[...]
    core_gather_wait(dens, 6)

    row = lax.broadcasted_iota(jnp.int32, (width, width), 0)
    col = lax.broadcasted_iota(jnp.int32, (width, width), 1)
    identity = jnp.where(row == col, 1.0, 0.0).astype(F32)
    density = dens[...]
    trace = jnp.sum(jnp.sum(density * identity, axis=0, keepdims=True), axis=1, keepdims=True)
    count = jnp.broadcast_to(rows_own, (1, 1)).astype(F32)
    shifted = density - (trace / count) * identity
    square = jnp.sum(jnp.sum(shifted * shifted, axis=0, keepdims=True), axis=1, keepdims=True)
    kept[...] = shifted / jnp.sqrt(square)

    @pl.loop(0, SIGN_STEPS)
    def _(step):
        current = kept[...]
        squared = jnp.dot(current, current, precision=lax.Precision.HIGHEST, preferred_element_type=F32)
        cubed = jnp.dot(squared, current, precision=lax.Precision.HIGHEST, preferred_element_type=F32)
        kept[...] = 1.5 * current - 0.5 * cubed

    kept[...] = 0.5 * (identity + kept[...])

    psi_copy.wait_send()

    @pl.loop(0, terms)
    def _(t):
        for copy in ops_copies(t):
            copy.wait_send()

    for copy in waits:
        if copy is not core_copy:
            copy.wait_send()


def per_device(zs, ns, tg, psi, left_ops, right_ops, left_dims, right_dims):
    terms, width = left_ops.shape[0], left_ops.shape[-1]
    half, xs = width // 2, tg // CORES
    quarter, ys = half // xs, ns // zs
    most = max(tg, zs, ys)
    vmem, smem = pl.BlockSpec(memory_space=pltpu.VMEM), pl.BlockSpec(memory_space=pltpu.SMEM)
    dma = pltpu.SemaphoreType.DMA
    state, kept, energy = pl.pallas_call(
        functools.partial(kernel, (ns, zs, tg, terms, width)),
        out_shape=(
            jax.ShapeDtypeStruct((3, width, width), BF16),
            jax.ShapeDtypeStruct((width, width), F32),
            jax.ShapeDtypeStruct((1, 1), F32),
        ),
        in_specs=[smem, smem, vmem, vmem, vmem],
        out_specs=(vmem, vmem, vmem),
        scratch_shapes=[pltpu.VMEM((terms, width, width), BF16)] * 4
        + [pltpu.VMEM((terms, width + 16, half), BF16)] * 4
        + [
            pltpu.VMEM((width, width), BF16),
            pltpu.VMEM((3, width, width), BF16),
            pltpu.VMEM((3, width, width), BF16),
            pltpu.VMEM((terms, 3, width, width), BF16),
            pltpu.VMEM((terms, 3, width, width), BF16),
            pltpu.VMEM((3, width, width), F32),
            pltpu.VMEM((2, width, width), F32),
            pltpu.VMEM((3, half, width), F32),
            pltpu.VMEM((2, half, width), F32),
            pltpu.VMEM((3, half, width), F32),
            pltpu.VMEM((2, half, width), F32),
            pltpu.VMEM((xs, 3, quarter, width), F32),
            pltpu.VMEM((xs, 2, quarter, width), F32),
            pltpu.VMEM((2, 3, most, 8, half), F32),
            pltpu.VMEM((8, half), F32),
            pltpu.VMEM((3, width, width), BF16),
            pltpu.VMEM((width, width), BF16),
            pltpu.VMEM((quarter, width), F32),
            pltpu.VMEM((quarter, width), F32),
            pltpu.VMEM((width, width), F32),
            dma((2, terms)),
            dma((2, terms)),
            dma((7,)),
            dma((7,)),
            dma((4, xs)),
            dma((4, xs)),
            dma((2, 3, most)),
            dma((2, 3, most)),
        ],
        compiler_params=pltpu.CompilerParams(
            collective_id=0, has_side_effects=True, vmem_limit_bytes=48 << 20
        ),
    )(left_dims, right_dims, psi[0], left_ops[:, 0], right_ops[:, 0])
    return state[None], kept[None], energy[0, 0]


def solution(mesh):
    ns, tg = mesh.shape["sec"], mesh.shape["term"]
    zs = ZSIZE if ns % ZSIZE == 0 and ns > ZSIZE else 2
    in_specs = (
        P("sec", None, None, None),
        P("term", "sec", None, None),
        P("term", "sec", None, None),
        P(),
        P(),
    )
    out_specs = (P("sec", None, None, None), P("sec", None, None), P())
    return jax.shard_map(
        functools.partial(per_device, zs, ns, tg),
        mesh=mesh, in_specs=in_specs, out_specs=out_specs, check_vma=False,
    )
```

time: 671 us -> 105 us (0.16); the launches traced: 659 us -> 105 us
  waiting for transfers between devices: 330 us -> 0 us
  blocking collectives: 234 us -> 0 us
  Pallas kernels: 0 us -> 97.2 us
  between operations: 32.3 us -> 2.35 us
  matrix products: 21.5 us -> 0 us
  other arithmetic: 20.5 us -> 0 us
  starting transfers between devices: 9.64 us -> 0 us
    psum x3 -> x0, waiting for transfers between devices: 262 us -> none  [the longest x2 171 us: reduce_whole(): return lax.psum(term_part, 'term')]
    psum x2 -> x0, blocking collectives: 234 us -> none  [sums_sector(): return lax.psum(values, 'sec')]
    pallas_call x0 -> x1, Pallas kernels: none -> 97.2 us  [per_device(): pl.pallas_call(functools.partial(kernel, (ns, zs, tg, terms, width)), out...]
    ppermute x4 -> x0, waiting for transfers between devices: 67.6 us -> none  [passed_along(): return lax.ppermute(value, axis, pairs)]
    dot_general x18 -> x0, matrix products: 21.5 us -> none  [the longest x1 8.51 us: per_device(): jnp.einsum('tkil,tkjl->kij', weighted, weighted, preferred_element_type=j...]
    convert_element_type x6 -> x0, other arithmetic: 12.4 us -> none  [the longest x2 6.15 us: symmetric(): widened = blocks.astype(jnp.float32)]
    ppermute x4 -> x0, starting transfers between devices: 9.52 us -> none  [passed_along(): return lax.ppermute(value, axis, pairs)]
    convert_element_type x2 -> x0, local copies, waits for them, and re-layouts: 8.46 us -> none  [symmetric(): widened = blocks.astype(jnp.float32)]
  transfers between devices with their start and end apart: 7 -> 0, of which waited for: 6 -> 0; matrix products, arithmetic and copies ran while one was open for 1% -> 0% of each run, Pallas kernels for 0% -> 0%
where the time goes in v1:
time: 105 us
  Pallas kernels  97.2 us (93%)
  local copies, waits for them, and re-layouts  5.55 us (5%)
  between operations  2.35 us (2%)
    pallas_call x1, Pallas kernels, per_device(): pl.pallas_call(functools.partial(kernel, (ns, zs, tg, terms, width)), out...  97.2 us
    unnamed x12, local copies, waits for them, and re-layouts  5.55 us

profile of v1, /device:TPU:1, one launch (start us, length us, event | category | flops | bytes accessed | tf_op | source)
XLA Modules:
  0.0 105.1 jit_solution(13369349491358208504)
XLA Ops:
  0.6 0.0 copy-start.3
  0.6 0.0 copy-start.4
  0.7 0.6 copy-done.3
  1.3 0.0 copy-done.4
  1.3 0.0 copy-start
  1.3 1.2 %copy-done = bf16[8,1,256,256]{3,2,1,0:T(8,128)(2,1)S(1)} copy-done((bf16[8,1,256,256]{3,2,1,0:T(8,128)(2,1)S(1)}, bf16[8,1,256,256]{3,2,1,0:T(8,128)(2,1)}, u32[]{:S(2)}) %copy-start) | copy-done | bytes 1048600
  2.5 0.0 copy-start.1
  2.5 1.2 %copy-done.1 = bf16[8,1,256,256]{3,2,1,0:T(8,128)(2,1)S(1)} copy-done((bf16[8,1,256,256]{3,2,1,0:T(8,128)(2,1)S(1)}, bf16[8,1,256,256]{3,2,1,0:T(8,128)(2,1)}, u32[]{:S(2)}) %copy-start.1) | copy-done | bytes 1048600
  3.8 0.0 copy-start.2
  3.8 1.0 copy-done.2
  4.8 97.2 %shard_map.76 = (bf16[3,256,256]{2,1,0:T(8,128)(2,1)S(1)}, f32[256,256]{1,0:T(8,128)S(1)}, f32[1,1]{1,0:T(1,128)}) custom-call(s32[64]{0:T(128)S(1)} %copy-done.3, s32[64]{0:T(128)S(1)} %copy-done.4, bf16[3,256,256]{2,1,0:T(8,128)(2,1)S(1)} %bitcast.8, bf16[8,256,256]{2,1,0:T(8,128)(2,1)S(1)} %bitcast.6, bf16[8,256,256]{2,1,0:T(8,128)(2,1)S(1)} %bitcast.7), custom_call_target="tpu_custom_call" | custom-call | tf_op jit(solution)/shard_map/pallas_call | solution.py:397
  101.9 0.7 copy.11
  102.7 0.7 copy.12
Async XLA Ops:
  0.6 0.7 copy-start.3
  0.6 0.7 copy-start.4
  1.3 1.2 %copy-start = (bf16[8,1,256,256]{3,2,1,0:T(8,128)(2,1)S(1)}, bf16[8,1,256,256]{3,2,1,0:T(8,128)(2,1)}, u32[]{:S(2)}) copy-start(bf16[8,1,256,256]{3,2,1,0:T(8,128)(2,1)} %param.6) | copy-start | bytes 3145732
  2.5 1.2 %copy-start.1 = (bf16[8,1,256,256]{3,2,1,0:T(8,128)(2,1)S(1)}, bf16[8,1,256,256]{3,2,1,0:T(8,128)(2,1)}, u32[]{:S(2)}) copy-start(bf16[8,1,256,256]{3,2,1,0:T(8,128)(2,1)} %param.7) | copy-start | bytes 3145732
  3.8 1.0 copy-start.2

commit v2 on v1

v2 whole, which is shorter than its diff:
```python
import functools

import jax
import jax.numpy as jnp
from jax import lax
from jax.experimental import pallas as pl
from jax.experimental.pallas import tpu as pltpu
from jax.sharding import PartitionSpec as P

SIGN_STEPS = 6
ZSIZE = 8
CORES = 2
NOISE_WEIGHT = 0.5
MESH = pl.DeviceIdType.MESH
F32 = jnp.float32
BF16 = jnp.bfloat16


def dot(a, b):
    return jnp.dot(a, b, preferred_element_type=F32)


def dot_t(a, b):
    return lax.dot_general(a, b, (((1,), (1,)), ((), ())), preferred_element_type=F32)


def halves(value):
    high = value.astype(BF16)
    return high, (value - high.astype(F32)).astype(BF16)


def dot_wide(a, b):
    (ah, al), (bh, bl) = a, b
    return dot(ah, bh) + (dot(ah, bl) + dot(al, bh))


def fold(value):
    half = value.shape[1] // 2
    row = jnp.sum(value, axis=0, keepdims=True)
    return row[:, :half] + row[:, half:]


def kernel(
    sizes,
    left_dims_hbm, right_dims_hbm, psi_hbm, left_hbm, right_hbm,
    new_state, kept, energy,
    left_dims, right_dims, psi, left, right,
    sl0, sr0, sl1, sr1, pack_l, pack_r, got_l, got_r, got_psi,
    vec, cor, img_a, img_b, acc, acc_b, core_a, half_a, part_a,
    n_one, n_two, mats, core_m, half_m, part_m, hop_out, hop_in, folded,
    sums, ns_two, ns_got,
    in_sem, pack_send, pack_recv, one_send, one_recv, c_send, c_recv, x_send, x_recv, s_send, s_recv,
):
    ns, zs, tg, terms, width = sizes
    ys, xs = ns // zs, tg // CORES
    half = width // 2
    me, lane = lax.axis_index("sec"), lax.axis_index("term")
    x, c = lax.div(lane, CORES), lax.rem(lane, CORES)
    y, z = lax.div(me, zs), lax.rem(me, zs)
    up, down = lax.rem(me + 1, ns), lax.rem(me + ns - 1, ns)
    partner = lane + 1 - 2 * c
    far_first = sorted(range(1, xs), key=lambda d: -min(d, xs - d))
    order = [lax.rem(x + d, xs) for d in far_first] + [x]

    def send(src, dst, ssem, rsem, sec, term):
        return pltpu.make_async_remote_copy(
            src_ref=src, dst_ref=dst, send_sem=ssem, recv_sem=rsem,
            device_id=(sec, term), device_id_type=MESH,
        )

    barrier = pltpu.get_barrier_semaphore()
    groups = [
        [((me, lax.rem(lane + d, tg)), lax.rem(lane + d, tg)) for d in range(1, tg)],
        [((y * zs + lax.rem(z + d, zs), lane), lax.rem(z + d, zs)) for d in range(1, zs)],
        [((lax.rem(y + d, ys) * zs + z, lane), lax.rem(y + d, ys)) for d in range(1, ys)],
    ]
    places = [lane, z, y]
    greeted = [peer for group in groups for peer, _ in group] + [(up, lane), (down, lane)]
    for peer in greeted:
        pl.semaphore_signal(barrier, inc=1, device_id=peer, device_id_type=MESH)

    def load_ops(t):
        return (
            pltpu.make_async_copy(left_hbm.at[t], left.at[t], in_sem.at[0, t]),
            pltpu.make_async_copy(right_hbm.at[t], right.at[t], in_sem.at[1, t]),
        )

    loads = [
        pltpu.make_async_copy(psi_hbm, psi, in_sem.at[2, 0]),
        pltpu.make_async_copy(left_dims_hbm, left_dims, in_sem.at[2, 1]),
        pltpu.make_async_copy(right_dims_hbm, right_dims, in_sem.at[3, 0]),
    ]
    for copy in load_ops(0):
        copy.start()
    for copy in loads:
        copy.start()
    for t in range(1, terms):
        for copy in load_ops(t):
            copy.start()

    row_h = lax.broadcasted_iota(jnp.int32, (half, half), 0)
    col_h = lax.broadcasted_iota(jnp.int32, (half, half), 1)

    def prepare(t, raw, sym, pack):
        wide = raw[t].astype(F32)
        whole = (wide + wide.T).astype(BF16)
        sym[t] = whole
        again = whole.astype(F32)
        low, high = again[:half, :half], again[half:, half:]
        pack[t, :half] = whole[:half, half:]
        pack[t, half:width] = jnp.where(row_h <= col_h, low, high).astype(BF16)
        diag = jnp.sum(jnp.where(row_h == col_h, high, 0.0), axis=0, keepdims=True)
        pack[t, width:] = jnp.broadcast_to(diag, (16, half)).astype(BF16)

    def restore(t, pack, sym):
        corner = pack[t, :half].astype(F32)
        mixed = pack[t, half:width].astype(F32)
        diag = pack[t, width:].astype(F32)[0:1]
        turned = mixed.T
        sym[t, :half, :half] = jnp.where(row_h <= col_h, mixed, turned).astype(BF16)
        sym[t, :half, half:] = pack[t, :half]
        sym[t, half:, :half] = corner.T.astype(BF16)
        lower = jnp.where(row_h == col_h, jnp.broadcast_to(diag, (half, half)), turned)
        sym[t, half:, half:] = jnp.where(row_h > col_h, mixed, lower).astype(BF16)

    def ops_copies(t):
        return (
            send(pack_l.at[t], got_l.at[t], pack_send.at[0, t], pack_recv.at[0, t], down, lane),
            send(pack_r.at[t], got_r.at[t], pack_send.at[1, t], pack_recv.at[1, t], up, lane),
        )

    def prepare_both(t):
        for copy in load_ops(t):
            copy.wait()
        prepare(t, left, sl0, pack_l)
        prepare(t, right, sr0, pack_r)

    waits = []

    def start(*copies):
        for copy in copies:
            copy.start()
        waits.extend(copies)

    def rows(ref, first, count):
        return ref.at[..., pl.ds(pl.multiple_of(first, count), count), :]

    def gather_start(ref, slot):
        hr, qr = ref.shape[-2] // 2, ref.shape[-2] // 2 // xs
        own = rows(ref, c * hr + x * qr, qr)
        for i, d in enumerate(far_first):
            start(send(own, own, x_send.at[slot, i], x_recv.at[slot, x], me, order[i] * CORES + c))
        start(send(own, own, c_send.at[slot, x], c_recv.at[slot, x], me, partner))

    def gather_pass(ref, slot):
        hr, qr = ref.shape[-2] // 2, ref.shape[-2] // 2 // xs
        for i in reversed(range(len(far_first))):
            piece = rows(ref, c * hr + order[i] * qr, qr)
            send(
                piece, piece, x_send.at[slot, i], x_recv.at[slot, order[i]], me, order[i] * CORES + c
            ).wait_recv()
            start(send(piece, piece, c_send.at[slot, order[i]], c_recv.at[slot, order[i]], me, partner))

    def gather_end(ref, slot):
        hr, qr = ref.shape[-2] // 2, ref.shape[-2] // 2 // xs
        for i in range(xs):
            piece = rows(ref, (1 - c) * hr + i * qr, qr)
            send(piece, piece, c_send.at[slot, i], c_recv.at[slot, i], me, partner).wait_recv()

    def core_copies(buf, core, slot):
        hr, qr = core.shape[-2], core.shape[-2] // xs
        return [
            send(
                rows(buf, (1 - c) * hr + xi * qr, qr), rows(core, xi * qr, qr),
                c_send.at[slot, i], c_recv.at[slot, i], me, partner,
            )
            for i, xi in enumerate(order)
        ]

    def scatter_start(buf, core, slot):
        start(*core_copies(buf, core, slot))

    def scatter_pass(buf, core, halved, part, slot):
        hr, qr = core.shape[-2], core.shape[-2] // xs
        copies = core_copies(buf, core, slot)
        late = None
        for i, xi in enumerate(order):
            copies[i].wait_recv()
            mine = rows(buf, c * hr + xi * qr, qr)[...] + rows(core, xi * qr, qr)[...]
            if i < xs - 1:
                piece = rows(halved, xi * qr, qr)
                piece[...] = mine
                now = send(
                    piece, part.at[x], x_send.at[slot, i], x_recv.at[slot, x], me, xi * CORES + c
                )
            else:
                part[x] = mine
                now = None
            if late is not None:
                start(late)
            late = now

    def scatter_end(halved, part, slot):
        qr = halved.shape[-2] // xs
        for i in range(xs - 1):
            send(
                rows(halved, order[i] * qr, qr), part.at[order[i]],
                x_send.at[slot, i], x_recv.at[slot, order[i]], me, order[i] * CORES + c,
            ).wait_recv()
        total = part[0]
        for i in range(1, xs):
            total = total + part[i]
        return total

    def scalar_start(rnd, stage, value):
        sums[rnd, stage, places[stage]] = value
        own = sums.at[rnd, stage, places[stage]]
        for d, (peer, _) in enumerate(groups[stage]):
            start(send(own, own, s_send.at[rnd, stage, d], s_recv.at[rnd, stage, places[stage]], *peer))

    def scalar_wait(rnd, stage):
        for d, (peer, place) in enumerate(groups[stage]):
            slot = sums.at[rnd, stage, place]
            send(slot, slot, s_send.at[rnd, stage, d], s_recv.at[rnd, stage, place], *peer).wait_recv()
        total = sums[rnd, stage, 0]
        for i in range(1, len(groups[stage]) + 1):
            total = total + sums[rnd, stage, i]
        return total

    def tile_of(values):
        values = values + [jnp.zeros((8 - len(values), half), F32)]
        return jnp.concatenate(values, axis=0)

    prepare_both(0)
    for copy in loads:
        copy.wait()
    pl.semaphore_wait(barrier, len(greeted))
    psi_rows = width // tg
    psi_piece = rows(got_psi, c * half + x * psi_rows, psi_rows)
    psi_copy = send(
        rows(psi.at[2], c * half + x * psi_rows, psi_rows), psi_piece,
        one_send.at[0], one_recv.at[0], up, lane,
    )
    start(psi_copy)

    @pl.loop(1, terms)
    def _(t):
        prepare_both(t)
        for copy in ops_copies(t - 1):
            copy.start()

    rows_own = left_dims[me]
    rows_next = jnp.where(me + 1 < ns, left_dims[up], 0)
    cols_own = right_dims[me]
    cols_last = jnp.where(me >= 1, right_dims[down], 0)
    live_rows = [rows_own, rows_next, rows_next]
    live_cols = [cols_own, cols_own, cols_last]

    def mask_of(k, first_row, count):
        row = lax.broadcasted_iota(jnp.int32, (count, width), 0) + first_row
        col = lax.broadcasted_iota(jnp.int32, (count, width), 1)
        return (row < live_rows[k]) & (col < live_cols[k])

    for k in range(2):
        vec[k] = jnp.where(mask_of(k, 0, width), psi[k].astype(F32), 0.0).astype(BF16)
    for copy in ops_copies(terms - 1):
        copy.start()
    psi_copy.wait_recv()
    gather_start(got_psi, 4)

    def part_own(t, blocks, images, total):
        image = dot(sl0[t], blocks[0]).astype(BF16)
        images[t, 0] = image
        total[0] += dot(image, sr0[t])

    def part_near(t, blocks, images, total):
        one = dot(sl1[t], blocks[1]).astype(BF16)
        two = dot(sl1[t], blocks[2]).astype(BF16)
        images[t, 1] = one
        images[t, 2] = two
        total[1] += dot(one, sr0[t])
        total[2] += dot(two, sr1[t])

    scale, each = NOISE_WEIGHT / (terms * tg), 1.0 / tg

    def grow(out, one, two, t, blocks):
        for k in blocks:
            out[min(k, 1)] += dot_t(one[t, k], two[t, k])

    def put_folded(slot, group, full):
        mats[slot, group, :half] = full[:half, :half]
        mats[slot, group, half:width] = full[:half, half:]
        mats[slot, group, width:] = full[half:, half:]

    acc[...] = jnp.zeros_like(acc)
    n_one[...] = jnp.zeros_like(n_one)

    @pl.loop(0, terms)
    def _(t):
        part_own(t, vec, img_a, acc)

    gather_pass(got_psi, 4)

    @pl.loop(0, terms)
    def _(t):
        grow(n_one, img_a, img_a, t, (0,))

    gather_end(got_psi, 4)
    vec[2] = jnp.where(mask_of(2, 0, width), got_psi[...].astype(F32), 0.0).astype(BF16)

    @pl.loop(0, terms)
    def _(t):
        for copy in ops_copies(t):
            copy.wait_recv()
        restore(t, got_l, sl1)
        restore(t, got_r, sr1)
        part_near(t, vec, img_a, acc)

        @pl.when(t > 0)
        def _():
            grow(n_one, img_a, img_a, t - 1, (1, 2))

    scatter_start(acc, core_a, 0)
    h11 = a11 = jnp.zeros((1, half), F32)
    for k in range(3):
        wide = vec[k].astype(F32)
        h11 = h11 + fold(wide * acc[k])
        a11 = a11 + fold(wide * wide)
    scalar_start(0, 0, tile_of([h11, a11]))
    scatter_pass(acc, core_a, half_a, part_a, 0)
    grow(n_one, img_a, img_a, terms - 1, (1, 2))
    put_folded(0, 0, scale * n_one[0] + each * dot_t(vec[0], vec[0]))
    put_folded(0, 1, scale * n_one[1] + each * (dot_t(vec[1], vec[1]) + dot_t(vec[2], vec[2])))
    acc_b[...] = jnp.zeros_like(acc_b)
    total = jnp.sum(scalar_wait(0, 0), axis=1, keepdims=True)
    h_here, a_here = total[0:1], total[1:2] * (1.0 / tg)
    some = a_here > 0.0
    level = jnp.where(some, h_here / jnp.where(some, a_here, 1.0), 0.0)
    shard = scatter_end(half_a, part_a, 0)
    quarter = half // xs
    own_row = pl.multiple_of(c * half + x * quarter, quarter)
    for k in range(3):
        held = vec[k, pl.ds(own_row, quarter), :].astype(F32)
        inside_k = jnp.where(mask_of(k, own_row, quarter), shard[k], 0.0)
        cor[k, pl.ds(own_row, quarter), :] = (inside_k - level * held).astype(BF16)
    gather_start(cor, 5)
    gather_pass(cor, 5)
    gather_end(cor, 5)
    scatter_start(mats.at[0], core_m.at[0], 1)

    @pl.loop(0, terms)
    def _(t):
        part_own(t, cor, img_b, acc_b)
        part_near(t, cor, img_b, acc_b)

    vc = cc = vhc = chc = jnp.zeros((1, half), F32)
    for k in range(3):
        wide, corr = vec[k].astype(F32), cor[k].astype(F32)
        summed = acc_b[k]
        vc = vc + fold(wide * corr)
        cc = cc + fold(corr * corr)
        vhc = vhc + fold(wide * summed)
        chc = chc + fold(corr * summed)
    scalar_start(1, 0, tile_of([
        a11 * (1.0 / tg),
        h11,
        (vc + level * a11) * (1.0 / tg),
        (cc + level * (2.0 * vc + level * a11)) * (1.0 / tg),
        vhc + level * h11,
        chc + level * (2.0 * vhc + level * h11),
    ]))
    scatter_pass(mats.at[0], core_m.at[0], half_m.at[0], part_m.at[0], 1)
    n_one[...] = jnp.zeros_like(n_one)
    n_two[...] = jnp.zeros_like(n_two)

    @pl.loop(0, terms)
    def _(t):
        grow(n_one, img_b, img_b, t, (0, 1, 2))

    put_folded(1, 0, scale * n_one[0] + each * dot_t(cor[0], cor[0]))
    put_folded(1, 1, scale * n_one[1] + each * (dot_t(cor[1], cor[1]) + dot_t(cor[2], cor[2])))
    scatter_start(mats.at[1], core_m.at[1], 2)
    scalar_start(1, 1, scalar_wait(1, 0))

    @pl.loop(0, terms)
    def _(t):
        grow(n_two, img_a, img_b, t, (0, 1, 2))

    cross = scale * n_two[0] + each * dot_t(vec[0], cor[0])
    put_folded(2, 0, cross + cross.T)
    cross = scale * n_two[1] + each * (dot_t(vec[1], cor[1]) + dot_t(vec[2], cor[2]))
    put_folded(2, 1, cross + cross.T)
    scatter_start(mats.at[2], core_m.at[2], 3)
    scatter_pass(mats.at[1], core_m.at[1], half_m.at[1], part_m.at[1], 2)
    scatter_pass(mats.at[2], core_m.at[2], half_m.at[2], part_m.at[2], 3)
    scalar_start(1, 2, scalar_wait(1, 1))
    shares = [scatter_end(half_m.at[q], part_m.at[q], 1 + q) for q in range(3)]
    count = shares[0].shape[1]
    for q in range(3):
        hop_out[q * count:(q + 1) * count] = shares[q][1]
    hop_out[3 * count:] = jnp.broadcast_to(level, (8, half))
    hop = send(hop_out, hop_in, one_send.at[1], one_recv.at[1], up, lane)
    start(hop)
    whole = jnp.sum(scalar_wait(1, 2), axis=1, keepdims=True)
    a11, h11 = whole[0:1], whole[1:2]
    mean = h11 / a11
    a12 = whole[2:3] - mean * a11
    a22 = whole[3:4] - mean * (2.0 * whole[2:3] - mean * a11)
    h12 = whole[4:5] - mean * h11
    h22 = whole[5:6] - mean * (2.0 * whole[4:5] - mean * h11)
    quad_a = a11 * a22 - a12 * a12
    quad_b = h11 * a22 + h22 * a11 - 2.0 * h12 * a12
    quad_c = h11 * h22 - h12 * h12
    lowest = (quad_b - jnp.sqrt(jnp.maximum(quad_b * quad_b - 4.0 * quad_a * quad_c, 0.0))) / (
        2.0 * quad_a
    )
    ratio = (lowest * a11 - h11) / (h12 - lowest * a12)
    first_coef = lax.rsqrt(a11 + 2.0 * ratio * a12 + ratio * ratio * a22)
    second_coef = ratio * first_coef
    energy[...] = lowest

    def weigh(coef, parts):
        return coef * coef * parts[0] + coef * second_coef * parts[2] + second_coef * second_coef * parts[1]

    coef = first_coef + second_coef * (level - mean)
    stay = weigh(coef, [shares[q][0] for q in range(3)])
    hop.wait_recv()
    coef_last = first_coef + second_coef * (hop_in[3 * count:3 * count + 1, 0:1] - mean)
    come = weigh(coef_last, [hop_in[q * count:(q + 1) * count] for q in range(3)])
    rows(folded, (c * xs + x) * count, count)[...] = stay + come
    ns_two[...] = (coef * vec[2].astype(F32) + second_coef * cor[2].astype(F32)).astype(BF16)
    gather_start(folded, 6)
    for k in range(2):
        new_state[k] = (coef * vec[k].astype(F32) + second_coef * cor[k].astype(F32)).astype(BF16)
    ns_copy = send(ns_two, ns_got, one_send.at[2], one_recv.at[2], down, lane)
    start(ns_copy)
    gather_pass(folded, 6)
    gather_end(folded, 6)

    row = lax.broadcasted_iota(jnp.int32, (width, width), 0)
    col = lax.broadcasted_iota(jnp.int32, (width, width), 1)
    identity = jnp.where(row == col, 1.0, 0.0).astype(F32)
    corner = folded[half:width]
    density = jnp.concatenate([
        jnp.concatenate([folded[:half], corner], axis=1),
        jnp.concatenate([corner.T, folded[width:]], axis=1),
    ], axis=0)
    density = jnp.where((row < rows_own) & (col < rows_own), density, 0.0)
    trace = jnp.sum(jnp.sum(density * identity, axis=0, keepdims=True), axis=1, keepdims=True)
    live = jnp.broadcast_to(rows_own, (1, 1)).astype(F32)
    shifted = density - (trace / live) * identity
    square = jnp.sum(jnp.sum(shifted * shifted, axis=0, keepdims=True), axis=1, keepdims=True)
    kept[...] = shifted / jnp.sqrt(square)

    @pl.loop(0, SIGN_STEPS)
    def _(step):
        current = kept[...]
        parts = halves(current)
        squared = dot_wide(parts, parts)
        cubed = dot_wide(halves(squared), parts)
        kept[...] = 1.5 * current - 0.5 * cubed

    kept[...] = 0.5 * (identity + kept[...])

    ns_copy.wait_recv()
    new_state[2] = ns_got[...]

    @pl.loop(0, terms)
    def _(t):
        for copy in ops_copies(t):
            copy.wait_send()

    for copy in waits:
        copy.wait_send()


def per_device(zs, ns, tg, psi, left_ops, right_ops, left_dims, right_dims):
    terms, width = left_ops.shape[0], left_ops.shape[-1]
    half, xs = width // 2, tg // CORES
    quarter, ys = half // xs, ns // zs
    tall = 3 * half
    share = tall // 2 // xs
    most = max(tg, zs, ys)
    vmem, hbm = pl.BlockSpec(memory_space=pltpu.VMEM), pl.BlockSpec(memory_space=pltpu.HBM)
    dma = pltpu.SemaphoreType.DMA
    state, kept, energy = pl.pallas_call(
        functools.partial(kernel, (ns, zs, tg, terms, width)),
        out_shape=(
            jax.ShapeDtypeStruct((3, width, width), BF16),
            jax.ShapeDtypeStruct((width, width), F32),
            jax.ShapeDtypeStruct((1, 1), F32),
        ),
        in_specs=[hbm] * 5,
        out_specs=(vmem, vmem, vmem),
        scratch_shapes=[pltpu.SMEM((ns,), jnp.int32)] * 2
        + [pltpu.VMEM((3, width, width), BF16)]
        + [pltpu.VMEM((terms, width, width), BF16)] * 6
        + [pltpu.VMEM((terms, width + 16, half), BF16)] * 4
        + [pltpu.VMEM((width, width), BF16)]
        + [pltpu.VMEM((3, width, width), BF16)] * 2
        + [pltpu.VMEM((terms, 3, width, width), BF16)] * 2
        + [pltpu.VMEM((3, width, width), F32)] * 2
        + [pltpu.VMEM((3, half, width), F32)] * 2
        + [pltpu.VMEM((xs, 3, quarter, width), F32)]
        + [pltpu.VMEM((2, width, width), F32)] * 2
        + [pltpu.VMEM((3, 2, tall, half), F32)]
        + [pltpu.VMEM((3, 2, tall // 2, half), F32)] * 2
        + [pltpu.VMEM((3, xs, 2, share, half), F32)]
        + [pltpu.VMEM((3 * share + 8, half), F32)] * 2
        + [pltpu.VMEM((tall, half), F32)]
        + [pltpu.VMEM((2, 3, most, 8, half), F32)]
        + [pltpu.VMEM((width, width), BF16)] * 2
        + [dma((4, terms)), dma((2, terms)), dma((2, terms)), dma((3,)), dma((3,))]
        + [dma((7, xs))] * 4
        + [dma((2, 3, most))] * 2,
        compiler_params=pltpu.CompilerParams(
            collective_id=0, has_side_effects=True, vmem_limit_bytes=48 << 20
        ),
    )(left_dims, right_dims, psi[0], left_ops[:, 0], right_ops[:, 0])
    return state[None], kept[None], energy[0, 0]


def solution(mesh):
    ns, tg = mesh.shape["sec"], mesh.shape["term"]
    zs = ZSIZE if ns % ZSIZE == 0 and ns > ZSIZE else 2
    in_specs = (
        P("sec", None, None, None),
        P("term", "sec", None, None),
        P("term", "sec", None, None),
        P(),
        P(),
    )
    out_specs = (P("sec", None, None, None), P("sec", None, None), P())
    return jax.shard_map(
        functools.partial(per_device, zs, ns, tg),
        mesh=mesh, in_specs=in_specs, out_specs=out_specs, check_vma=False,
    )
```

time: 105 us -> 86.7 us (0.83)
  Pallas kernels: 97.2 us -> 78.5 us
    pallas_call x1, Pallas kernels: 97.2 us -> 78.5 us  [per_device(): pl.pallas_call(functools.partial(kernel, (ns, zs, tg, terms, width)), out...]
where the time goes in v2:
time: 86.7 us; the launch traced here: 86.4 us
  Pallas kernels  78.5 us (91%)
  local copies, waits for them, and re-layouts  5.55 us (6%)
  between operations  2.35 us (3%)
    pallas_call x1, Pallas kernels, per_device(): pl.pallas_call(functools.partial(kernel, (ns, zs, tg, terms, width)), out...  78.5 us
    unnamed x12, local copies, waits for them, and re-layouts  5.55 us

profile of v2, /device:TPU:1, one launch (start us, length us, event | category | flops | bytes accessed | tf_op | source)
XLA Modules:
  0.0 86.4 jit_solution(9312184016859970154)
XLA Ops:
  0.6 0.0 copy-start.3
  0.6 0.0 copy-start.4
  0.7 0.6 copy-done.3
  1.3 0.0 copy-done.4
  1.3 0.0 copy-start
  1.3 1.2 %copy-done = bf16[8,1,256,256]{3,2,1,0:T(8,128)(2,1)S(1)} copy-done((bf16[8,1,256,256]{3,2,1,0:T(8,128)(2,1)S(1)}, bf16[8,1,256,256]{3,2,1,0:T(8,128)(2,1)}, u32[]{:S(2)}) %copy-start) | copy-done | bytes 1048600
  2.5 0.0 copy-start.1
  2.5 1.2 %copy-done.1 = bf16[8,1,256,256]{3,2,1,0:T(8,128)(2,1)S(1)} copy-done((bf16[8,1,256,256]{3,2,1,0:T(8,128)(2,1)S(1)}, bf16[8,1,256,256]{3,2,1,0:T(8,128)(2,1)}, u32[]{:S(2)}) %copy-start.1) | copy-done | bytes 1048600
  3.8 0.0 copy-start.2
  3.8 1.0 %copy-done.2 = bf16[1,3,256,256]{3,2,1,0:T(8,128)(2,1)S(1)} copy-done((bf16[1,3,256,256]{3,2,1,0:T(8,128)(2,1)S(1)}, bf16[1,3,256,256]{3,2,1,0:T(8,128)(2,1)}, u32[]{:S(2)}) %copy-start.2) | copy-done | bytes 393240
  4.8 78.5 %shard_map.76 = (bf16[3,256,256]{2,1,0:T(8,128)(2,1)S(1)}, f32[256,256]{1,0:T(8,128)S(1)}, f32[1,1]{1,0:T(1,128)}) custom-call(s32[64]{0:T(128)S(1)} %copy-done.3, s32[64]{0:T(128)S(1)} %copy-done.4, bf16[3,256,256]{2,1,0:T(8,128)(2,1)S(1)} %bitcast.8, bf16[8,256,256]{2,1,0:T(8,128)(2,1)S(1)} %bitcast.6, bf16[8,256,256]{2,1,0:T(8,128)(2,1)S(1)} %bitcast.7), custom_call_target="tpu_custom_call" | custom-call | tf_op jit(solution)/shard_map/pallas_call | solution.py:486
  83.3 0.7 copy.11
  84.0 0.7 copy.12
Async XLA Ops:
  0.6 0.7 copy-start.3
  0.6 0.7 copy-start.4
  1.3 1.2 %copy-start = (bf16[8,1,256,256]{3,2,1,0:T(8,128)(2,1)S(1)}, bf16[8,1,256,256]{3,2,1,0:T(8,128)(2,1)}, u32[]{:S(2)}) copy-start(bf16[8,1,256,256]{3,2,1,0:T(8,128)(2,1)} %param.6) | copy-start | bytes 3145732
  2.5 1.2 %copy-start.1 = (bf16[8,1,256,256]{3,2,1,0:T(8,128)(2,1)S(1)}, bf16[8,1,256,256]{3,2,1,0:T(8,128)(2,1)}, u32[]{:S(2)}) copy-start(bf16[8,1,256,256]{3,2,1,0:T(8,128)(2,1)} %param.7) | copy-start | bytes 3145732
  3.8 1.0 %copy-start.2 = (bf16[1,3,256,256]{3,2,1,0:T(8,128)(2,1)S(1)}, bf16[1,3,256,256]{3,2,1,0:T(8,128)(2,1)}, u32[]{:S(2)}) copy-start(bf16[1,3,256,256]{3,2,1,0:T(8,128)(2,1)} %param.5) | copy-start | bytes 1179652

commit v3 on v2

--- a/solution.py
+++ b/solution.py
@@ -31,7 +31,7 @@
 
 def dot_wide(a, b):
     (ah, al), (bh, bl) = a, b
-    return dot(ah, bh) + (dot(ah, bl) + dot(al, bh))
+    return dot(jnp.concatenate([ah, ah, al], axis=1), jnp.concatenate([bh, bl, bh], axis=0))
 
 
 def fold(value):
@@ -46,8 +46,8 @@
     new_state, kept, energy,
     left_dims, right_dims, psi, left, right,
     sl0, sr0, sl1, sr1, pack_l, pack_r, got_l, got_r, got_psi,
-    vec, cor, img_a, img_b, acc, acc_b, core_a, half_a, part_a,
-    n_one, n_two, mats, core_m, half_m, part_m, hop_out, hop_in, folded,
+    vec, cor, img_a, img_b, acc, acc_b, core_a, half_a, part_a, part_b,
+    nacc, mats, core_m, half_m, part_m, part_n, hop_out, hop_in, folded,
     sums, ns_two, ns_got,
     in_sem, pack_send, pack_recv, one_send, one_recv, c_send, c_recv, x_send, x_recv, s_send, s_recv,
 ):
@@ -79,24 +79,21 @@
     for peer in greeted:
         pl.semaphore_signal(barrier, inc=1, device_id=peer, device_id_type=MESH)
 
-    def load_ops(t):
-        return (
-            pltpu.make_async_copy(left_hbm.at[t], left.at[t], in_sem.at[0, t]),
-            pltpu.make_async_copy(right_hbm.at[t], right.at[t], in_sem.at[1, t]),
-        )
-
+    def load(src, dst, slot):
+        return pltpu.make_async_copy(src, dst, in_sem.at[slot])
+
+    rest = pl.ds(1, terms - 1)
     loads = [
-        pltpu.make_async_copy(psi_hbm, psi, in_sem.at[2, 0]),
-        pltpu.make_async_copy(left_dims_hbm, left_dims, in_sem.at[2, 1]),
-        pltpu.make_async_copy(right_dims_hbm, right_dims, in_sem.at[3, 0]),
+        load(left_hbm.at[0], left.at[0], 0),
+        load(right_hbm.at[0], right.at[0], 1),
+        load(psi_hbm, psi, 2),
+        load(left_hbm.at[rest], left.at[rest], 3),
+        load(right_hbm.at[rest], right.at[rest], 4),
+        load(left_dims_hbm, left_dims, 5),
+        load(right_dims_hbm, right_dims, 6),
     ]
-    for copy in load_ops(0):
-        copy.start()
     for copy in loads:
         copy.start()
-    for t in range(1, terms):
-        for copy in load_ops(t):
-            copy.start()
 
     row_h = lax.broadcasted_iota(jnp.int32, (half, half), 0)
     col_h = lax.broadcasted_iota(jnp.int32, (half, half), 1)
@@ -130,8 +127,6 @@
         )
 
     def prepare_both(t):
-        for copy in load_ops(t):
-            copy.wait()
         prepare(t, left, sl0, pack_l)
         prepare(t, right, sr0, pack_r)
 
@@ -231,9 +226,10 @@
         values = values + [jnp.zeros((8 - len(values), half), F32)]
         return jnp.concatenate(values, axis=0)
 
+    loads[0].wait()
+    loads[1].wait()
     prepare_both(0)
-    for copy in loads:
-        copy.wait()
+    loads[2].wait()
     pl.semaphore_wait(barrier, len(greeted))
     psi_rows = width // tg
     psi_piece = rows(got_psi, c * half + x * psi_rows, psi_rows)
@@ -242,6 +238,8 @@
         one_send.at[0], one_recv.at[0], up, lane,
     )
     start(psi_copy)
+    for copy in loads[3:]:
+        copy.wait()
 
     @pl.loop(1, terms)
     def _(t):
@@ -265,143 +263,222 @@
         vec[k] = jnp.where(mask_of(k, 0, width), psi[k].astype(F32), 0.0).astype(BF16)
     for copy in ops_copies(terms - 1):
         copy.start()
-    psi_copy.wait_recv()
-    gather_start(got_psi, 4)
+
+    scale, each = NOISE_WEIGHT / (terms * tg), 1.0 / tg
+    quarter = half // xs
+    own_row = pl.multiple_of(c * half + x * quarter, quarter)
+    teams = [(0,), (1, 2)]
 
     def part_own(t, blocks, images, total):
         image = dot(sl0[t], blocks[0]).astype(BF16)
         images[t, 0] = image
         total[0] += dot(image, sr0[t])
 
-    def part_near(t, blocks, images, total):
-        one = dot(sl1[t], blocks[1]).astype(BF16)
-        two = dot(sl1[t], blocks[2]).astype(BF16)
-        images[t, 1] = one
-        images[t, 2] = two
-        total[1] += dot(one, sr0[t])
-        total[2] += dot(two, sr1[t])
-
-    scale, each = NOISE_WEIGHT / (terms * tg), 1.0 / tg
-
-    def grow(out, one, two, t, blocks):
-        for k in blocks:
-            out[min(k, 1)] += dot_t(one[t, k], two[t, k])
-
-    def put_folded(slot, group, full):
-        mats[slot, group, :half] = full[:half, :half]
-        mats[slot, group, half:width] = full[:half, half:]
-        mats[slot, group, width:] = full[half:, half:]
-
-    acc[...] = jnp.zeros_like(acc)
-    n_one[...] = jnp.zeros_like(n_one)
-
-    @pl.loop(0, terms)
-    def _(t):
-        part_own(t, vec, img_a, acc)
-
-    gather_pass(got_psi, 4)
-
-    @pl.loop(0, terms)
-    def _(t):
-        grow(n_one, img_a, img_a, t, (0,))
-
-    gather_end(got_psi, 4)
-    vec[2] = jnp.where(mask_of(2, 0, width), got_psi[...].astype(F32), 0.0).astype(BF16)
-
-    @pl.loop(0, terms)
-    def _(t):
+    def part_one(t, blocks, images, total):
+        image = dot(sl1[t], blocks[1]).astype(BF16)
+        images[t, 1] = image
+        total[1] += dot(image, sr0[t])
+
+    def part_two(t, blocks, images, total):
+        image = dot(sl1[t], blocks[2]).astype(BF16)
+        images[t, 2] = image
+        total[2] += dot(image, sr1[t])
+
+    def grow(slot, team, one, two, t):
+        for k in teams[team]:
+            nacc[team, slot] += dot_t(one[t, k], two[t, k])
+
+    def put_folded(slot, team, full):
+        mats[team, slot, :half] = full[:half, :half]
+        mats[team, slot, half:width] = full[:half, half:]
+        mats[team, slot, width:] = full[half:, half:]
+
+    def own_part(team, one, two):
+        total = dot_t(one[teams[team][0]], two[teams[team][0]])
+        for k in teams[team][1:]:
+            total = total + dot_t(one[k], two[k])
+        return each * total
+
+    def put_plain(slot, team, one):
+        put_folded(slot, team, scale * nacc[team, slot] + own_part(team, one, one))
+
+    def put_cross(slot, team, one, two):
+        cross = scale * nacc[team, slot] + own_part(team, one, two)
+        put_folded(slot, team, cross + cross.T)
+
+    def norms(team):
+        h_row = a_row = jnp.zeros((1, half), F32)
+        for k in teams[team]:
+            wide = vec[k].astype(F32)
+            h_row = h_row + fold(wide * acc[k])
+            a_row = a_row + fold(wide * wide)
+        return h_row, a_row
+
+    def level_of(rnd):
+        total = jnp.sum(scalar_wait(rnd, 0), axis=1, keepdims=True)
+        h_here, a_here = total[0:1], total[1:2] * each
+        some = a_here > 0.0
+        return jnp.where(some, h_here / jnp.where(some, a_here, 1.0), 0.0)
+
+    def correct(team, level, shard):
+        for i, k in enumerate(teams[team]):
+            held = vec[k, pl.ds(own_row, quarter), :].astype(F32)
+            inside_k = jnp.where(mask_of(k, own_row, quarter), shard[i], 0.0)
+            cor[k, pl.ds(own_row, quarter), :] = (inside_k - level * held).astype(BF16)
+
+    near = pl.ds(1, 2)
+    acc_of = [acc.at[pl.ds(0, 1)], acc.at[near]]
+    core_of = [core_a.at[pl.ds(0, 1)], core_a.at[near]]
+    half_of = [half_a.at[pl.ds(0, 1)], half_a.at[near]]
+    part_of = [part_a, part_b]
+    cor_of = [cor.at[pl.ds(0, 1)], cor.at[near]]
+
+    def arrive(t):
         for copy in ops_copies(t):
             copy.wait_recv()
         restore(t, got_l, sl1)
         restore(t, got_r, sr1)
-        part_near(t, vec, img_a, acc)
-
-        @pl.when(t > 0)
-        def _():
-            grow(n_one, img_a, img_a, t - 1, (1, 2))
-
-    scatter_start(acc, core_a, 0)
-    h11 = a11 = jnp.zeros((1, half), F32)
-    for k in range(3):
-        wide = vec[k].astype(F32)
-        h11 = h11 + fold(wide * acc[k])
-        a11 = a11 + fold(wide * wide)
-    scalar_start(0, 0, tile_of([h11, a11]))
-    scatter_pass(acc, core_a, half_a, part_a, 0)
-    grow(n_one, img_a, img_a, terms - 1, (1, 2))
-    put_folded(0, 0, scale * n_one[0] + each * dot_t(vec[0], vec[0]))
-    put_folded(0, 1, scale * n_one[1] + each * (dot_t(vec[1], vec[1]) + dot_t(vec[2], vec[2])))
+
+    acc[...] = jnp.zeros_like(acc)
     acc_b[...] = jnp.zeros_like(acc_b)
-    total = jnp.sum(scalar_wait(0, 0), axis=1, keepdims=True)
-    h_here, a_here = total[0:1], total[1:2] * (1.0 / tg)
-    some = a_here > 0.0
-    level = jnp.where(some, h_here / jnp.where(some, a_here, 1.0), 0.0)
-    shard = scatter_end(half_a, part_a, 0)
-    quarter = half // xs
-    own_row = pl.multiple_of(c * half + x * quarter, quarter)
-    for k in range(3):
-        held = vec[k, pl.ds(own_row, quarter), :].astype(F32)
-        inside_k = jnp.where(mask_of(k, own_row, quarter), shard[k], 0.0)
-        cor[k, pl.ds(own_row, quarter), :] = (inside_k - level * held).astype(BF16)
-    gather_start(cor, 5)
-    gather_pass(cor, 5)
-    gather_end(cor, 5)
-    scatter_start(mats.at[0], core_m.at[0], 1)
-
-    @pl.loop(0, terms)
+    nacc[...] = jnp.zeros_like(nacc)
+
+    @pl.loop(0, terms, unroll=True)
+    def _(t):
+        part_own(t, vec, img_a, acc)
+
+    scatter_start(acc_of[0], core_of[0], 0)
+    h_zero, a_zero = norms(0)
+    scalar_start(0, 0, tile_of([h_zero, a_zero]))
+    psi_copy.wait_recv()
+    gather_start(got_psi, 8)
+    scatter_pass(acc_of[0], core_of[0], half_of[0], part_of[0], 0)
+
+    @pl.loop(0, terms, unroll=True)
+    def _(t):
+        grow(0, 0, img_a, img_a, t)
+
+    early = terms // 4
+    for t in range(early):
+        arrive(t)
+        part_one(t, vec, img_a, acc)
+    gather_pass(got_psi, 8)
+    level_zero = level_of(0)
+    shard = scatter_end(half_of[0], part_of[0], 0)
+    correct(0, level_zero, shard)
+    gather_start(cor_of[0], 9)
+    gather_end(got_psi, 8)
+    vec[2] = jnp.where(mask_of(2, 0, width), got_psi[...].astype(F32), 0.0).astype(BF16)
+    for t in range(early):
+        part_two(t, vec, img_a, acc)
+    middle = terms // 2
+    for t in range(early, middle):
+        arrive(t)
+        part_one(t, vec, img_a, acc)
+        part_two(t, vec, img_a, acc)
+    gather_pass(cor_of[0], 9)
+    for t in range(middle, middle + 1):
+        arrive(t)
+        part_one(t, vec, img_a, acc)
+        part_two(t, vec, img_a, acc)
+    gather_end(cor_of[0], 9)
+
+    @pl.loop(0, terms, unroll=True)
     def _(t):
         part_own(t, cor, img_b, acc_b)
-        part_near(t, cor, img_b, acc_b)
-
-    vc = cc = vhc = chc = jnp.zeros((1, half), F32)
-    for k in range(3):
-        wide, corr = vec[k].astype(F32), cor[k].astype(F32)
-        summed = acc_b[k]
-        vc = vc + fold(wide * corr)
-        cc = cc + fold(corr * corr)
-        vhc = vhc + fold(wide * summed)
-        chc = chc + fold(corr * summed)
-    scalar_start(1, 0, tile_of([
-        a11 * (1.0 / tg),
-        h11,
-        (vc + level * a11) * (1.0 / tg),
-        (cc + level * (2.0 * vc + level * a11)) * (1.0 / tg),
-        vhc + level * h11,
-        chc + level * (2.0 * vhc + level * h11),
-    ]))
-    scatter_pass(mats.at[0], core_m.at[0], half_m.at[0], part_m.at[0], 1)
-    n_one[...] = jnp.zeros_like(n_one)
-    n_two[...] = jnp.zeros_like(n_two)
-
-    @pl.loop(0, terms)
-    def _(t):
-        grow(n_one, img_b, img_b, t, (0, 1, 2))
-
-    put_folded(1, 0, scale * n_one[0] + each * dot_t(cor[0], cor[0]))
-    put_folded(1, 1, scale * n_one[1] + each * (dot_t(cor[1], cor[1]) + dot_t(cor[2], cor[2])))
-    scatter_start(mats.at[1], core_m.at[1], 2)
-    scalar_start(1, 1, scalar_wait(1, 0))
-
-    @pl.loop(0, terms)
-    def _(t):
-        grow(n_two, img_a, img_b, t, (0, 1, 2))
-
-    cross = scale * n_two[0] + each * dot_t(vec[0], cor[0])
-    put_folded(2, 0, cross + cross.T)
-    cross = scale * n_two[1] + each * (dot_t(vec[1], cor[1]) + dot_t(vec[2], cor[2]))
-    put_folded(2, 1, cross + cross.T)
-    scatter_start(mats.at[2], core_m.at[2], 3)
-    scatter_pass(mats.at[1], core_m.at[1], half_m.at[1], part_m.at[1], 2)
-    scatter_pass(mats.at[2], core_m.at[2], half_m.at[2], part_m.at[2], 3)
-    scalar_start(1, 2, scalar_wait(1, 1))
-    shares = [scatter_end(half_m.at[q], part_m.at[q], 1 + q) for q in range(3)]
-    count = shares[0].shape[1]
+
+    for t in range(middle + 1, terms):
+        arrive(t)
+        part_one(t, vec, img_a, acc)
+        part_two(t, vec, img_a, acc)
+    scatter_start(acc_of[1], core_of[1], 1)
+    h_near, a_near = norms(1)
+    scalar_start(1, 0, tile_of([h_near, a_near]))
+
+    @pl.loop(0, terms, unroll=True)
+    def _(t):
+        grow(1, 0, img_b, img_b, t)
+
+    scatter_pass(acc_of[1], core_of[1], half_of[1], part_of[1], 1)
+
+    @pl.loop(0, terms, unroll=True)
+    def _(t):
+        grow(2, 0, img_a, img_b, t)
+
+    put_plain(0, 0, vec)
+    put_plain(1, 0, cor)
+    put_cross(2, 0, vec, cor)
+    scatter_start(mats.at[0], core_m.at[0], 2)
+    level_near = level_of(1)
+    shard = scatter_end(half_of[1], part_of[1], 1)
+    correct(1, level_near, shard)
+    gather_start(cor_of[1], 10)
+
+    @pl.loop(0, terms, unroll=True)
+    def _(t):
+        grow(0, 1, img_a, img_a, t)
+
+    put_plain(0, 1, vec)
+    scatter_start(mats.at[1, 0], core_m.at[1, 0], 3)
+    gather_pass(cor_of[1], 10)
+    gather_end(cor_of[1], 10)
+
+    scatter_pass(mats.at[0], core_m.at[0], half_m.at[0], part_m, 2)
+
+    @pl.loop(0, terms, unroll=True)
+    def _(t):
+        part_one(t, cor, img_b, acc_b)
+        part_two(t, cor, img_b, acc_b)
+
+    levels = [level_zero, level_near]
+    sides = [(h_zero, a_zero), (h_near, a_near)]
+    tile = 0.0
+    for team in range(2):
+        level, (h_row, a_row) = levels[team], sides[team]
+        vc = cc = vhc = chc = jnp.zeros((1, half), F32)
+        for k in teams[team]:
+            wide, corr = vec[k].astype(F32), cor[k].astype(F32)
+            summed = acc_b[k]
+            vc = vc + fold(wide * corr)
+            cc = cc + fold(corr * corr)
+            vhc = vhc + fold(wide * summed)
+            chc = chc + fold(corr * summed)
+        tile = tile + tile_of([
+            a_row * each,
+            h_row,
+            (vc + level * a_row) * each,
+            (cc + level * (2.0 * vc + level * a_row)) * each,
+            vhc + level * h_row,
+            chc + level * (2.0 * vhc + level * h_row),
+        ])
+    scalar_start(2, 0, tile)
+    scatter_pass(mats.at[1, 0], core_m.at[1, 0], half_m.at[1, 0], part_n.at[0], 3)
+
+    @pl.loop(0, terms, unroll=True)
+    def _(t):
+        grow(1, 1, img_b, img_b, t)
+
+    put_plain(1, 1, cor)
+    scatter_start(mats.at[1, 1], core_m.at[1, 1], 4)
+
+    @pl.loop(0, terms, unroll=True)
+    def _(t):
+        grow(2, 1, img_a, img_b, t)
+
+    put_cross(2, 1, vec, cor)
+    scatter_start(mats.at[1, 2], core_m.at[1, 2], 5)
+    scatter_pass(mats.at[1, 1], core_m.at[1, 1], half_m.at[1, 1], part_n.at[1], 4)
+    scalar_start(2, 1, scalar_wait(2, 0))
+    scatter_pass(mats.at[1, 2], core_m.at[1, 2], half_m.at[1, 2], part_n.at[2], 5)
+    stay = scatter_end(half_m.at[0], part_m, 2)
+    count = stay.shape[1]
     for q in range(3):
-        hop_out[q * count:(q + 1) * count] = shares[q][1]
-    hop_out[3 * count:] = jnp.broadcast_to(level, (8, half))
+        hop_out[q * count:(q + 1) * count] = scatter_end(half_m.at[1, q], part_n.at[q], 3 + q)
+    hop_out[3 * count:] = jnp.broadcast_to(level_near, (8, half))
     hop = send(hop_out, hop_in, one_send.at[1], one_recv.at[1], up, lane)
     start(hop)
-    whole = jnp.sum(scalar_wait(1, 2), axis=1, keepdims=True)
+    scalar_start(2, 2, scalar_wait(2, 1))
+    whole = jnp.sum(scalar_wait(2, 2), axis=1, keepdims=True)
     a11, h11 = whole[0:1], whole[1:2]
     mean = h11 / a11
     a12 = whole[2:3] - mean * a11
@@ -422,20 +499,20 @@
     def weigh(coef, parts):
         return coef * coef * parts[0] + coef * second_coef * parts[2] + second_coef * second_coef * parts[1]
 
-    coef = first_coef + second_coef * (level - mean)
-    stay = weigh(coef, [shares[q][0] for q in range(3)])
+    coefs = [first_coef + second_coef * (level - mean) for level in levels]
+    stay = weigh(coefs[0], [stay[q] for q in range(3)])
     hop.wait_recv()
     coef_last = first_coef + second_coef * (hop_in[3 * count:3 * count + 1, 0:1] - mean)
     come = weigh(coef_last, [hop_in[q * count:(q + 1) * count] for q in range(3)])
     rows(folded, (c * xs + x) * count, count)[...] = stay + come
-    ns_two[...] = (coef * vec[2].astype(F32) + second_coef * cor[2].astype(F32)).astype(BF16)
-    gather_start(folded, 6)
+    ns_two[...] = (coefs[1] * vec[2].astype(F32) + second_coef * cor[2].astype(F32)).astype(BF16)
+    gather_start(folded, 11)
     for k in range(2):
-        new_state[k] = (coef * vec[k].astype(F32) + second_coef * cor[k].astype(F32)).astype(BF16)
+        new_state[k] = (coefs[k] * vec[k].astype(F32) + second_coef * cor[k].astype(F32)).astype(BF16)
     ns_copy = send(ns_two, ns_got, one_send.at[2], one_recv.at[2], down, lane)
     start(ns_copy)
-    gather_pass(folded, 6)
-    gather_end(folded, 6)
+    gather_pass(folded, 11)
+    gather_end(folded, 11)
 
     row = lax.broadcasted_iota(jnp.int32, (width, width), 0)
     col = lax.broadcasted_iota(jnp.int32, (width, width), 1)
@@ -501,20 +578,22 @@
         + [pltpu.VMEM((terms, 3, width, width), BF16)] * 2
         + [pltpu.VMEM((3, width, width), F32)] * 2
         + [pltpu.VMEM((3, half, width), F32)] * 2
-        + [pltpu.VMEM((xs, 3, quarter, width), F32)]
-        + [pltpu.VMEM((2, width, width), F32)] * 2
-        + [pltpu.VMEM((3, 2, tall, half), F32)]
-        + [pltpu.VMEM((3, 2, tall // 2, half), F32)] * 2
-        + [pltpu.VMEM((3, xs, 2, share, half), F32)]
+        + [pltpu.VMEM((xs, 1, quarter, width), F32)]
+        + [pltpu.VMEM((xs, 2, quarter, width), F32)]
+        + [pltpu.VMEM((2, 3, width, width), F32)]
+        + [pltpu.VMEM((2, 3, tall, half), F32)]
+        + [pltpu.VMEM((2, 3, tall // 2, half), F32)] * 2
+        + [pltpu.VMEM((xs, 3, share, half), F32)]
+        + [pltpu.VMEM((3, xs, share, half), F32)]
         + [pltpu.VMEM((3 * share + 8, half), F32)] * 2
         + [pltpu.VMEM((tall, half), F32)]
-        + [pltpu.VMEM((2, 3, most, 8, half), F32)]
+        + [pltpu.VMEM((3, 3, most, 8, half), F32)]
         + [pltpu.VMEM((width, width), BF16)] * 2
-        + [dma((4, terms)), dma((2, terms)), dma((2, terms)), dma((3,)), dma((3,))]
-        + [dma((7, xs))] * 4
-        + [dma((2, 3, most))] * 2,
+        + [dma((7,)), dma((2, terms)), dma((2, terms)), dma((3,)), dma((3,))]
+        + [dma((12, xs))] * 4
+        + [dma((3, 3, most))] * 2,
         compiler_params=pltpu.CompilerParams(
-            collective_id=0, has_side_effects=True, vmem_limit_bytes=48 << 20
+            collective_id=0, has_side_effects=True, vmem_limit_bytes=67043328
         ),
     )(left_dims, right_dims, psi[0], left_ops[:, 0], right_ops[:, 0])
     return state[None], kept[None], energy[0, 0]

time: 86.7 us -> 77.8 us (0.90)
  Pallas kernels: 78.5 us -> 72.6 us
  local copies, waits for them, and re-layouts: 5.55 us -> 2.52 us
    pallas_call x1, Pallas kernels: 78.5 us -> 72.6 us  [per_device(): pl.pallas_call(functools.partial(kernel, (ns, zs, tg, terms, width)), out...]
    unnamed x12 -> x4, local copies, waits for them, and re-layouts: 5.55 us -> 2.52 us
where the time goes in v3:
time: 77.8 us; the launch traced here: 77.6 us
  Pallas kernels  72.6 us (93%)
  local copies, waits for them, and re-layouts  2.52 us (3%)
  between operations  2.41 us (3%)
    pallas_call x1, Pallas kernels, per_device(): pl.pallas_call(functools.partial(kernel, (ns, zs, tg, terms, width)), out...  72.6 us
    unnamed x4, local copies, waits for them, and re-layouts  2.52 us

profile of v3, /device:TPU:1, one launch (start us, length us, event | category | flops | bytes accessed | tf_op | source)
XLA Modules:
  0.0 77.6 jit_solution(7986945735380557381)
XLA Ops:
  0.6 72.6 %shard_map.76 = (bf16[3,256,256]{2,1,0:T(8,128)(2,1)}, f32[256,256]{1,0:T(8,128)}, f32[1,1]{1,0:T(1,128)}) custom-call(s32[64]{0:T(128)} %left_dims_hbm.1, s32[64]{0:T(128)} %right_dims_hbm.1, bf16[3,256,256]{2,1,0:T(8,128)(2,1)} %bitcast.8, bf16[8,256,256]{2,1,0:T(8,128)(2,1)} %bitcast.6, bf16[8,256,256]{2,1,0:T(8,128)(2,1)} %bitcast.7), custom_call_target="tpu_custom_call" | custom-call | tf_op jit(solution)/shard_map/pallas_call | solution.py:563
  73.3 0.0 copy-start
  73.3 1.8 %copy.11 = bf16[1,3,256,256]{3,2,1,0:T(8,128)(2,1)} copy(bf16[1,3,256,256]{3,2,1,0:T(8,128)(2,1)} %bitcast.9) | data formatting | bytes 786432
  75.1 0.0 copy-done
  75.1 0.7 copy.12
Async XLA Ops:
  73.3 1.8 %copy-start = (f32[256,256]{1,0:T(8,128)S(1)}, f32[256,256]{1,0:T(8,128)}, u32[]{:S(2)}) copy-start(f32[256,256]{1,0:T(8,128)} %get-tuple-element.7) | copy-start | bytes 786436

commit v4 on v3

--- a/solution.py
+++ b/solution.py
@@ -43,12 +43,12 @@
 def kernel(
     sizes,
     left_dims_hbm, right_dims_hbm, psi_hbm, left_hbm, right_hbm,
-    new_state, kept, energy,
+    state_hbm, folded_hbm,
     left_dims, right_dims, psi, left, right,
     sl0, sr0, sl1, sr1, pack_l, pack_r, got_l, got_r, got_psi,
-    vec, cor, img_a, img_b, acc, acc_b, core_a, half_a, part_a, part_b,
+    vec, cor, img_a, img_b, acc, acc_b, core_a, half_a, part_a,
     nacc, mats, core_m, half_m, part_m, part_n, hop_out, hop_in, folded,
-    sums, ns_two, ns_got,
+    sums, ns_mine, cor_got, tag_out, tag_in,
     in_sem, pack_send, pack_recv, one_send, one_recv, c_send, c_recv, x_send, x_recv, s_send, s_recv,
 ):
     ns, zs, tg, terms, width = sizes
@@ -107,7 +107,7 @@
         pack[t, :half] = whole[:half, half:]
         pack[t, half:width] = jnp.where(row_h <= col_h, low, high).astype(BF16)
         diag = jnp.sum(jnp.where(row_h == col_h, high, 0.0), axis=0, keepdims=True)
-        pack[t, width:] = jnp.broadcast_to(diag, (16, half)).astype(BF16)
+        pack[t, width:] = jnp.broadcast_to(diag, (8, half)).astype(BF16)
 
     def restore(t, pack, sym):
         corner = pack[t, :half].astype(F32)
@@ -222,9 +222,15 @@
             total = total + sums[rnd, stage, i]
         return total
 
-    def tile_of(values):
-        values = values + [jnp.zeros((8 - len(values), half), F32)]
-        return jnp.concatenate(values, axis=0)
+    one_hot = lax.broadcasted_iota(jnp.int32, (8, half), 0) == lax.broadcasted_iota(jnp.int32, (8, half), 1)
+
+    def row_of(values):
+        values = jnp.concatenate(values + [jnp.zeros((8 - len(values), half), F32)], axis=0)
+        full = jnp.broadcast_to(jnp.sum(values, axis=1, keepdims=True), (8, half))
+        return jnp.sum(jnp.where(one_hot, full, 0.0), axis=0, keepdims=True)
+
+    def column_of(row):
+        return jnp.sum(jnp.where(one_hot, jnp.broadcast_to(row, (8, half)), 0.0), axis=1, keepdims=True)
 
     loads[0].wait()
     loads[1].wait()
@@ -315,23 +321,21 @@
         return h_row, a_row
 
     def level_of(rnd):
-        total = jnp.sum(scalar_wait(rnd, 0), axis=1, keepdims=True)
+        total = column_of(scalar_wait(rnd, 0))
         h_here, a_here = total[0:1], total[1:2] * each
         some = a_here > 0.0
         return jnp.where(some, h_here / jnp.where(some, a_here, 1.0), 0.0)
 
-    def correct(team, level, shard):
-        for i, k in enumerate(teams[team]):
-            held = vec[k, pl.ds(own_row, quarter), :].astype(F32)
-            inside_k = jnp.where(mask_of(k, own_row, quarter), shard[i], 0.0)
-            cor[k, pl.ds(own_row, quarter), :] = (inside_k - level * held).astype(BF16)
-
-    near = pl.ds(1, 2)
-    acc_of = [acc.at[pl.ds(0, 1)], acc.at[near]]
-    core_of = [core_a.at[pl.ds(0, 1)], core_a.at[near]]
-    half_of = [half_a.at[pl.ds(0, 1)], half_a.at[near]]
-    part_of = [part_a, part_b]
-    cor_of = [cor.at[pl.ds(0, 1)], cor.at[near]]
+    def correct(k, level, shard):
+        held = vec[k, pl.ds(own_row, quarter), :].astype(F32)
+        inside_k = jnp.where(mask_of(k, own_row, quarter), shard[0], 0.0)
+        cor[k, pl.ds(own_row, quarter), :] = (inside_k - level * held).astype(BF16)
+
+    acc_of = [acc.at[pl.ds(k, 1)] for k in range(3)]
+    core_of = [core_a.at[pl.ds(k, 1)] for k in range(3)]
+    half_of = [half_a.at[pl.ds(k, 1)] for k in range(3)]
+    part_of = [part_a.at[k] for k in range(3)]
+    cor_of = [cor.at[pl.ds(k, 1)] for k in range(3)]
 
     def arrive(t):
         for copy in ops_copies(t):
@@ -349,7 +353,7 @@
 
     scatter_start(acc_of[0], core_of[0], 0)
     h_zero, a_zero = norms(0)
-    scalar_start(0, 0, tile_of([h_zero, a_zero]))
+    scalar_start(0, 0, row_of([h_zero, a_zero]))
     psi_copy.wait_recv()
     gather_start(got_psi, 8)
     scatter_pass(acc_of[0], core_of[0], half_of[0], part_of[0], 0)
@@ -392,14 +396,16 @@
         part_one(t, vec, img_a, acc)
         part_two(t, vec, img_a, acc)
     scatter_start(acc_of[1], core_of[1], 1)
+    scatter_start(acc_of[2], core_of[2], 6)
     h_near, a_near = norms(1)
-    scalar_start(1, 0, tile_of([h_near, a_near]))
+    scalar_start(1, 0, row_of([h_near, a_near]))
 
     @pl.loop(0, terms, unroll=True)
     def _(t):
         grow(1, 0, img_b, img_b, t)
 
     scatter_pass(acc_of[1], core_of[1], half_of[1], part_of[1], 1)
+    scatter_pass(acc_of[2], core_of[2], half_of[2], part_of[2], 6)
 
     @pl.loop(0, terms, unroll=True)
     def _(t):
@@ -413,6 +419,9 @@
     shard = scatter_end(half_of[1], part_of[1], 1)
     correct(1, level_near, shard)
     gather_start(cor_of[1], 10)
+    shard = scatter_end(half_of[2], part_of[2], 6)
+    correct(2, level_near, shard)
+    gather_start(cor_of[2], 7)
 
     @pl.loop(0, terms, unroll=True)
     def _(t):
@@ -423,16 +432,27 @@
     gather_pass(cor_of[1], 10)
     gather_end(cor_of[1], 10)
 
+    @pl.loop(0, middle, unroll=True)
+    def _(t):
+        part_one(t, cor, img_b, acc_b)
+
+    gather_pass(cor_of[2], 7)
+
+    @pl.loop(middle, terms, unroll=True)
+    def _(t):
+        part_one(t, cor, img_b, acc_b)
+
+    gather_end(cor_of[2], 7)
+    tag_out[...] = jnp.broadcast_to(level_near, (8, half))
     scatter_pass(mats.at[0], core_m.at[0], half_m.at[0], part_m, 2)
 
     @pl.loop(0, terms, unroll=True)
     def _(t):
-        part_one(t, cor, img_b, acc_b)
         part_two(t, cor, img_b, acc_b)
 
     levels = [level_zero, level_near]
     sides = [(h_zero, a_zero), (h_near, a_near)]
-    tile = 0.0
+    gathered = [jnp.zeros((1, half), F32)] * 6
     for team in range(2):
         level, (h_row, a_row) = levels[team], sides[team]
         vc = cc = vhc = chc = jnp.zeros((1, half), F32)
@@ -443,15 +463,16 @@
             cc = cc + fold(corr * corr)
             vhc = vhc + fold(wide * summed)
             chc = chc + fold(corr * summed)
-        tile = tile + tile_of([
+        here = [
             a_row * each,
             h_row,
             (vc + level * a_row) * each,
             (cc + level * (2.0 * vc + level * a_row)) * each,
             vhc + level * h_row,
             chc + level * (2.0 * vhc + level * h_row),
-        ])
-    scalar_start(2, 0, tile)
+        ]
+        gathered = [one + two for one, two in zip(gathered, here)]
+    scalar_start(2, 1, row_of(gathered))
     scatter_pass(mats.at[1, 0], core_m.at[1, 0], half_m.at[1, 0], part_n.at[0], 3)
 
     @pl.loop(0, terms, unroll=True)
@@ -468,7 +489,12 @@
     put_cross(2, 1, vec, cor)
     scatter_start(mats.at[1, 2], core_m.at[1, 2], 5)
     scatter_pass(mats.at[1, 1], core_m.at[1, 1], half_m.at[1, 1], part_n.at[1], 4)
-    scalar_start(2, 1, scalar_wait(2, 0))
+    scalar_start(2, 2, scalar_wait(2, 1))
+    to_owner = [
+        send(cor.at[2], cor_got, one_send.at[2], one_recv.at[2], down, lane),
+        send(tag_out, tag_in, one_send.at[3], one_recv.at[3], down, lane),
+    ]
+    start(*to_owner)
     scatter_pass(mats.at[1, 2], core_m.at[1, 2], half_m.at[1, 2], part_n.at[2], 5)
     stay = scatter_end(half_m.at[0], part_m, 2)
     count = stay.shape[1]
@@ -477,14 +503,14 @@
     hop_out[3 * count:] = jnp.broadcast_to(level_near, (8, half))
     hop = send(hop_out, hop_in, one_send.at[1], one_recv.at[1], up, lane)
     start(hop)
-    scalar_start(2, 2, scalar_wait(2, 1))
-    whole = jnp.sum(scalar_wait(2, 2), axis=1, keepdims=True)
-    a11, h11 = whole[0:1], whole[1:2]
+    scalar_start(2, 0, scalar_wait(2, 2))
+    whole = column_of(scalar_wait(2, 0))
+    a11, h11, v_u, u_u, v_hu, u_hu = [whole[q:q + 1] for q in range(6)]
     mean = h11 / a11
-    a12 = whole[2:3] - mean * a11
-    a22 = whole[3:4] - mean * (2.0 * whole[2:3] - mean * a11)
-    h12 = whole[4:5] - mean * h11
-    h22 = whole[5:6] - mean * (2.0 * whole[4:5] - mean * h11)
+    a12 = v_u - mean * a11
+    a22 = u_u - mean * (2.0 * v_u - mean * a11)
+    h12 = v_hu - mean * h11
+    h22 = u_hu - mean * (2.0 * v_hu - mean * h11)
     quad_a = a11 * a22 - a12 * a12
     quad_b = h11 * a22 + h22 * a11 - 2.0 * h12 * a12
     quad_c = h11 * h22 - h12 * h12
@@ -494,7 +520,6 @@
     ratio = (lowest * a11 - h11) / (h12 - lowest * a12)
     first_coef = lax.rsqrt(a11 + 2.0 * ratio * a12 + ratio * ratio * a22)
     second_coef = ratio * first_coef
-    energy[...] = lowest
 
     def weigh(coef, parts):
         return coef * coef * parts[0] + coef * second_coef * parts[2] + second_coef * second_coef * parts[1]
@@ -504,51 +529,74 @@
     hop.wait_recv()
     coef_last = first_coef + second_coef * (hop_in[3 * count:3 * count + 1, 0:1] - mean)
     come = weigh(coef_last, [hop_in[q * count:(q + 1) * count] for q in range(3)])
-    rows(folded, (c * xs + x) * count, count)[...] = stay + come
-    ns_two[...] = (coefs[1] * vec[2].astype(F32) + second_coef * cor[2].astype(F32)).astype(BF16)
-    gather_start(folded, 11)
-    for k in range(2):
-        new_state[k] = (coefs[k] * vec[k].astype(F32) + second_coef * cor[k].astype(F32)).astype(BF16)
-    ns_copy = send(ns_two, ns_got, one_send.at[2], one_recv.at[2], down, lane)
-    start(ns_copy)
-    gather_pass(folded, 11)
-    gather_end(folded, 11)
-
+    piled = folded.at[pl.ds(0, 3 * half)]
+    rows(piled, (c * xs + x) * count, count)[...] = stay + come
+    gather_start(piled, 11)
+    for copy in to_owner:
+        copy.wait_recv()
+    coefs.append(first_coef + second_coef * (tag_in[0:1, 0:1] - mean))
+    rows_last = jnp.where(me + 2 < ns, left_dims[lax.rem(me + 2, ns)], 0)
+    row = lax.broadcasted_iota(jnp.int32, (width, width), 0)
+    col = lax.broadcasted_iota(jnp.int32, (width, width), 1)
+    last = jnp.where((row < rows_last) & (col < cols_own), psi[2].astype(F32), 0.0)
+    pairs = [(vec[k].astype(F32), cor[k].astype(F32)) for k in range(2)] + [(last, cor_got[...].astype(F32))]
+    for k, (wide, corr) in enumerate(pairs):
+        ns_mine[k] = (coefs[k] * wide + second_coef * corr).astype(BF16)
+    tail = lax.broadcasted_iota(jnp.int32, (8, half), 0)
+    live = jnp.broadcast_to(rows_own, (8, half)).astype(F32)
+    folded[3 * half:] = jnp.where(tail == 0, live, lowest)
+    state_copy = load(ns_mine, state_hbm, 7)
+    state_copy.start()
+    gather_pass(piled, 11)
+    gather_end(piled, 11)
+    folded_copy = load(folded, folded_hbm, 8)
+    folded_copy.start()
+    @pl.loop(0, terms)
+    def _(t):
+        for copy in ops_copies(t):
+            copy.wait_send()
+
+    for copy in waits:
+        copy.wait_send()
+    state_copy.wait()
+    folded_copy.wait()
+
+
+def sign_kernel(half, folded, state_hbm, new_state_hbm, kept, energy, state, sem):
+    width = 2 * half
+    into = pltpu.make_async_copy(state_hbm, state, sem.at[0])
+    into.start()
     row = lax.broadcasted_iota(jnp.int32, (width, width), 0)
     col = lax.broadcasted_iota(jnp.int32, (width, width), 1)
     identity = jnp.where(row == col, 1.0, 0.0).astype(F32)
+    live = folded[3 * half:3 * half + 1, 0:1]
+    energy[...] = folded[3 * half + 1:3 * half + 2, 0:1]
     corner = folded[half:width]
     density = jnp.concatenate([
         jnp.concatenate([folded[:half], corner], axis=1),
-        jnp.concatenate([corner.T, folded[width:]], axis=1),
+        jnp.concatenate([corner.T, folded[width:3 * half]], axis=1),
     ], axis=0)
-    density = jnp.where((row < rows_own) & (col < rows_own), density, 0.0)
+    inside = (row.astype(F32) < live) & (col.astype(F32) < live)
+    density = jnp.where(inside, density, 0.0)
     trace = jnp.sum(jnp.sum(density * identity, axis=0, keepdims=True), axis=1, keepdims=True)
-    live = jnp.broadcast_to(rows_own, (1, 1)).astype(F32)
     shifted = density - (trace / live) * identity
     square = jnp.sum(jnp.sum(shifted * shifted, axis=0, keepdims=True), axis=1, keepdims=True)
     kept[...] = shifted / jnp.sqrt(square)
-
-    @pl.loop(0, SIGN_STEPS)
-    def _(step):
+    out = pltpu.make_async_copy(state, new_state_hbm, sem.at[1])
+
+    def step():
         current = kept[...]
         parts = halves(current)
         squared = dot_wide(parts, parts)
         cubed = dot_wide(halves(squared), parts)
         kept[...] = 1.5 * current - 0.5 * cubed
 
+    pl.loop(0, SIGN_STEPS // 2)(lambda _: step())
+    into.wait()
+    out.start()
+    pl.loop(SIGN_STEPS // 2, SIGN_STEPS)(lambda _: step())
     kept[...] = 0.5 * (identity + kept[...])
-
-    ns_copy.wait_recv()
-    new_state[2] = ns_got[...]
-
-    @pl.loop(0, terms)
-    def _(t):
-        for copy in ops_copies(t):
-            copy.wait_send()
-
-    for copy in waits:
-        copy.wait_send()
+    out.wait()
 
 
 def per_device(zs, ns, tg, psi, left_ops, right_ops, left_dims, right_dims):
@@ -560,43 +608,53 @@
     most = max(tg, zs, ys)
     vmem, hbm = pl.BlockSpec(memory_space=pltpu.VMEM), pl.BlockSpec(memory_space=pltpu.HBM)
     dma = pltpu.SemaphoreType.DMA
-    state, kept, energy = pl.pallas_call(
+    state, folded = pl.pallas_call(
         functools.partial(kernel, (ns, zs, tg, terms, width)),
         out_shape=(
             jax.ShapeDtypeStruct((3, width, width), BF16),
-            jax.ShapeDtypeStruct((width, width), F32),
-            jax.ShapeDtypeStruct((1, 1), F32),
+            jax.ShapeDtypeStruct((tall + 8, half), F32),
         ),
         in_specs=[hbm] * 5,
-        out_specs=(vmem, vmem, vmem),
+        out_specs=(hbm, hbm),
         scratch_shapes=[pltpu.SMEM((ns,), jnp.int32)] * 2
         + [pltpu.VMEM((3, width, width), BF16)]
         + [pltpu.VMEM((terms, width, width), BF16)] * 6
-        + [pltpu.VMEM((terms, width + 16, half), BF16)] * 4
+        + [pltpu.VMEM((terms, width + 8, half), BF16)] * 4
         + [pltpu.VMEM((width, width), BF16)]
         + [pltpu.VMEM((3, width, width), BF16)] * 2
         + [pltpu.VMEM((terms, 3, width, width), BF16)] * 2
         + [pltpu.VMEM((3, width, width), F32)] * 2
         + [pltpu.VMEM((3, half, width), F32)] * 2
-        + [pltpu.VMEM((xs, 1, quarter, width), F32)]
-        + [pltpu.VMEM((xs, 2, quarter, width), F32)]
+        + [pltpu.VMEM((3, xs, 1, quarter, width), F32)]
         + [pltpu.VMEM((2, 3, width, width), F32)]
         + [pltpu.VMEM((2, 3, tall, half), F32)]
         + [pltpu.VMEM((2, 3, tall // 2, half), F32)] * 2
         + [pltpu.VMEM((xs, 3, share, half), F32)]
         + [pltpu.VMEM((3, xs, share, half), F32)]
         + [pltpu.VMEM((3 * share + 8, half), F32)] * 2
-        + [pltpu.VMEM((tall, half), F32)]
-        + [pltpu.VMEM((3, 3, most, 8, half), F32)]
-        + [pltpu.VMEM((width, width), BF16)] * 2
-        + [dma((7,)), dma((2, terms)), dma((2, terms)), dma((3,)), dma((3,))]
+        + [pltpu.VMEM((tall + 8, half), F32)]
+        + [pltpu.VMEM((3, 3, most, 1, half), F32)]
+        + [pltpu.VMEM((3, width, width), BF16), pltpu.VMEM((width, width), BF16)]
+        + [pltpu.VMEM((8, half), F32)] * 2
+        + [dma((9,)), dma((2, terms)), dma((2, terms)), dma((4,)), dma((4,))]
         + [dma((12, xs))] * 4
         + [dma((3, 3, most))] * 2,
         compiler_params=pltpu.CompilerParams(
             collective_id=0, has_side_effects=True, vmem_limit_bytes=67043328
         ),
     )(left_dims, right_dims, psi[0], left_ops[:, 0], right_ops[:, 0])
-    return state[None], kept[None], energy[0, 0]
+    new_state, kept, energy = pl.pallas_call(
+        functools.partial(sign_kernel, half),
+        out_shape=(
+            jax.ShapeDtypeStruct((3, width, width), BF16),
+            jax.ShapeDtypeStruct((width, width), F32),
+            jax.ShapeDtypeStruct((1, 1), F32),
+        ),
+        in_specs=[vmem, hbm],
+        out_specs=(hbm, vmem, vmem),
+        scratch_shapes=[pltpu.VMEM((3, width, width), BF16), dma((2,))],
+    )(folded, state)
+    return new_state[None], kept[None], energy[0, 0]
 
 
 def solution(mesh):

time: 77.8 us -> 72 us (0.925)
  local copies, waits for them, and re-layouts: 2.52 us -> 0 us
  between operations: 2.41 us -> 0.64 us
  Pallas kernels: 72.6 us -> 71.2 us
    pallas_call x1, Pallas kernels: 72.6 us -> 65.5 us  [per_device(): pl.pallas_call(functools.partial(kernel, (ns, zs, tg, terms, width)), out...]
    pallas_call x0 -> x1, Pallas kernels: none -> 5.7 us  [per_device(): pl.pallas_call(functools.partial(sign_kernel, half), out_shape=(jax.Shape...]
    unnamed x4 -> x0, local copies, waits for them, and re-layouts: 2.52 us -> none
where the time goes in v4:
time: 72 us; the launch traced here: 71.8 us
  Pallas kernels  71.2 us (99%)
    pallas_call x1, Pallas kernels, per_device(): pl.pallas_call(functools.partial(kernel, (ns, zs, tg, terms, width)), out...  65.5 us
    pallas_call x1, Pallas kernels, per_device(): pl.pallas_call(functools.partial(sign_kernel, half), out_shape=(jax.Shape...  5.7 us

profile of v4, /device:TPU:1, one launch (start us, length us, event | category | flops | bytes accessed | tf_op | source)
XLA Modules:
  0.0 71.8 jit_solution(6367182965723443874)
XLA Ops:
  0.6 65.5 %shard_map.76 = (bf16[3,256,256]{2,1,0:T(8,128)(2,1)}, f32[392,128]{1,0:T(8,128)}) custom-call(s32[64]{0:T(128)} %left_dims_hbm.1, s32[64]{0:T(128)} %right_dims_hbm.1, bf16[3,256,256]{2,1,0:T(8,128)(2,1)} %bitcast.8, bf16[8,256,256]{2,1,0:T(8,128)(2,1)} %bitcast.6, bf16[8,256,256]{2,1,0:T(8,128)(2,1)} %bitcast.7), custom_call_target="tpu_custom_call" | custom-call | tf_op jit(solution)/shard_map/pallas_call | solution.py:611
  66.1 5.7 %shard_map.77 = (bf16[3,256,256]{2,1,0:T(8,128)(2,1)}, f32[256,256]{1,0:T(8,128)}, f32[1,1]{1,0:T(1,128)}) custom-call(f32[392,128]{1,0:T(8,128)} %get-tuple-element.8.folded, bf16[3,256,256]{2,1,0:T(8,128)(2,1)} %get-tuple-element.9.state_hbm), custom_call_target="tpu_custom_call" | custom-call | tf_op jit(solution)/shard_map/pallas_call | solution.py:646

commit v5 on v4

--- a/solution.py
+++ b/solution.py
@@ -49,7 +49,7 @@
     vec, cor, img_a, img_b, acc, acc_b, core_a, half_a, part_a,
     nacc, mats, core_m, half_m, part_m, part_n, hop_out, hop_in, folded,
     sums, ns_mine, cor_got, tag_out, tag_in,
-    in_sem, pack_send, pack_recv, one_send, one_recv, c_send, c_recv, x_send, x_recv, s_send, s_recv,
+    in_sem, pack_send, pack_recv, one_send, one_recv, c_send, c_recv, x_send, x_recv, s_send, s_recv, chain,
 ):
     ns, zs, tg, terms, width = sizes
     ys, xs = ns // zs, tg // CORES
@@ -75,9 +75,28 @@
         [((lax.rem(y + d, ys) * zs + z, lane), lax.rem(y + d, ys)) for d in range(1, ys)],
     ]
     places = [lane, z, y]
-    greeted = [peer for group in groups for peer, _ in group] + [(up, lane), (down, lane)]
+    rings = [
+        [(y * zs + lax.rem(z + 1, zs), lane), (y * zs + lax.rem(z + zs - 1, zs), lane)],
+        [(lax.rem(y + 1, ys) * zs + z, lane), (lax.rem(y + ys - 1, ys) * zs + z, lane)],
+    ]
+    reach = [zs // 2 - 1, ys // 2 - 1]
+    greeted = [peer for peer, _ in groups[0]] + rings[0] + rings[1] + [(up, lane), (down, lane)]
     for peer in greeted:
         pl.semaphore_signal(barrier, inc=1, device_id=peer, device_id_type=MESH)
+
+    def vouch(turn):
+        for axis in range(2):
+            if turn < reach[axis]:
+                for side, peer in enumerate(rings[axis]):
+                    pl.semaphore_signal(
+                        chain.at[axis, turn, side], inc=1, device_id=peer, device_id_type=MESH
+                    )
+
+    def vouched(turn):
+        for axis in range(2):
+            if turn < reach[axis]:
+                for side in range(2):
+                    pl.semaphore_wait(chain.at[axis, turn, side], 1)
 
     def load(src, dst, slot):
         return pltpu.make_async_copy(src, dst, in_sem.at[slot])
@@ -237,6 +256,7 @@
     prepare_both(0)
     loads[2].wait()
     pl.semaphore_wait(barrier, len(greeted))
+    vouch(0)
     psi_rows = width // tg
     psi_piece = rows(got_psi, c * half + x * psi_rows, psi_rows)
     psi_copy = send(
@@ -366,6 +386,8 @@
     for t in range(early):
         arrive(t)
         part_one(t, vec, img_a, acc)
+    vouched(0)
+    vouch(1)
     gather_pass(got_psi, 8)
     level_zero = level_of(0)
     shard = scatter_end(half_of[0], part_of[0], 0)
@@ -380,6 +402,8 @@
         arrive(t)
         part_one(t, vec, img_a, acc)
         part_two(t, vec, img_a, acc)
+    vouched(1)
+    vouch(2)
     gather_pass(cor_of[0], 9)
     for t in range(middle, middle + 1):
         arrive(t)
@@ -391,6 +415,9 @@
     def _(t):
         part_own(t, cor, img_b, acc_b)
 
+    for turn in range(2, max(reach)):
+        vouched(turn)
+        vouch(turn + 1)
     for t in range(middle + 1, terms):
         arrive(t)
         part_one(t, vec, img_a, acc)
@@ -432,15 +459,15 @@
     gather_pass(cor_of[1], 10)
     gather_end(cor_of[1], 10)
 
-    @pl.loop(0, middle, unroll=True)
+    @pl.loop(0, terms, unroll=True)
     def _(t):
         part_one(t, cor, img_b, acc_b)
 
     gather_pass(cor_of[2], 7)
 
-    @pl.loop(middle, terms, unroll=True)
-    def _(t):
-        part_one(t, cor, img_b, acc_b)
+    @pl.loop(0, terms, unroll=True)
+    def _(t):
+        nacc[1, 1] += dot_t(img_b[t, 1], img_b[t, 1])
 
     gather_end(cor_of[2], 7)
     tag_out[...] = jnp.broadcast_to(level_near, (8, half))
@@ -477,7 +504,7 @@
 
     @pl.loop(0, terms, unroll=True)
     def _(t):
-        grow(1, 1, img_b, img_b, t)
+        nacc[1, 1] += dot_t(img_b[t, 2], img_b[t, 2])
 
     put_plain(1, 1, cor)
     scatter_start(mats.at[1, 1], core_m.at[1, 1], 4)
@@ -496,6 +523,7 @@
     ]
     start(*to_owner)
     scatter_pass(mats.at[1, 2], core_m.at[1, 2], half_m.at[1, 2], part_n.at[2], 5)
+    scalar_start(2, 0, scalar_wait(2, 2))
     stay = scatter_end(half_m.at[0], part_m, 2)
     count = stay.shape[1]
     for q in range(3):
@@ -503,7 +531,6 @@
     hop_out[3 * count:] = jnp.broadcast_to(level_near, (8, half))
     hop = send(hop_out, hop_in, one_send.at[1], one_recv.at[1], up, lane)
     start(hop)
-    scalar_start(2, 0, scalar_wait(2, 2))
     whole = column_of(scalar_wait(2, 0))
     a11, h11, v_u, u_u, v_hu, u_hu = [whole[q:q + 1] for q in range(6)]
     mean = h11 / a11
@@ -638,7 +665,8 @@
         + [pltpu.VMEM((8, half), F32)] * 2
         + [dma((9,)), dma((2, terms)), dma((2, terms)), dma((4,)), dma((4,))]
         + [dma((12, xs))] * 4
-        + [dma((3, 3, most))] * 2,
+        + [dma((3, 3, most))] * 2
+        + [pltpu.SemaphoreType.REGULAR((2, max(zs // 2, ys // 2), 2))],
         compiler_params=pltpu.CompilerParams(
             collective_id=0, has_side_effects=True, vmem_limit_bytes=67043328
         ),

time: 72 us -> 72.1 us (level)
  no operation moved by 1% of the time
where the time goes in v5:
time: 72.1 us; the launch traced here: 72 us
  Pallas kernels  71.3 us (99%)
    pallas_call x1, Pallas kernels, per_device(): pl.pallas_call(functools.partial(kernel, (ns, zs, tg, terms, width)), out...  65.6 us
    pallas_call x1, Pallas kernels, per_device(): pl.pallas_call(functools.partial(sign_kernel, half), out_shape=(jax.Shape...  5.7 us

profile of v5, /device:TPU:1, one launch (start us, length us, event | category | flops | bytes accessed | tf_op | source)
XLA Modules:
  0.0 72.0 jit_solution(15525924424192371326)
XLA Ops:
  0.6 65.6 %shard_map.76 = (bf16[3,256,256]{2,1,0:T(8,128)(2,1)}, f32[392,128]{1,0:T(8,128)}) custom-call(s32[64]{0:T(128)} %left_dims_hbm.1, s32[64]{0:T(128)} %right_dims_hbm.1, bf16[3,256,256]{2,1,0:T(8,128)(2,1)} %bitcast.8, bf16[8,256,256]{2,1,0:T(8,128)(2,1)} %bitcast.6, bf16[8,256,256]{2,1,0:T(8,128)(2,1)} %bitcast.7), custom_call_target="tpu_custom_call" | custom-call | tf_op jit(solution)/shard_map/pallas_call | solution.py:638
  66.3 5.7 %shard_map.77 = (bf16[3,256,256]{2,1,0:T(8,128)(2,1)}, f32[256,256]{1,0:T(8,128)}, f32[1,1]{1,0:T(1,128)}) custom-call(f32[392,128]{1,0:T(8,128)} %get-tuple-element.8.folded, bf16[3,256,256]{2,1,0:T(8,128)(2,1)} %get-tuple-element.9.state_hbm), custom_call_target="tpu_custom_call" | custom-call | tf_op jit(solution)/shard_map/pallas_call | solution.py:674

commit v6 on v5

--- a/solution.py
+++ b/solution.py
@@ -29,9 +29,8 @@
     return high, (value - high.astype(F32)).astype(BF16)
 
 
-def dot_wide(a, b):
-    (ah, al), (bh, bl) = a, b
-    return dot(jnp.concatenate([ah, ah, al], axis=1), jnp.concatenate([bh, bl, bh], axis=0))
+def beside(high, low):
+    return jnp.concatenate([high, high, low], axis=1)
 
 
 def fold(value):
@@ -49,7 +48,8 @@
     vec, cor, img_a, img_b, acc, acc_b, core_a, half_a, part_a,
     nacc, mats, core_m, half_m, part_m, part_n, hop_out, hop_in, folded,
     sums, ns_mine, cor_got, tag_out, tag_in,
-    in_sem, pack_send, pack_recv, one_send, one_recv, c_send, c_recv, x_send, x_recv, s_send, s_recv, chain,
+    in_sem, pack_send, pack_recv, one_send, one_recv, sum_core, sum_core_in, sum_x, sum_x_in,
+    all_core, all_core_in, all_x, all_x_in, s_send, s_recv, chain,
 ):
     ns, zs, tg, terms, width = sizes
     ys, xs = ns // zs, tg // CORES
@@ -81,9 +81,6 @@
     ]
     reach = [zs // 2 - 1, ys // 2 - 1]
     greeted = [peer for peer, _ in groups[0]] + rings[0] + rings[1] + [(up, lane), (down, lane)]
-    for peer in greeted:
-        pl.semaphore_signal(barrier, inc=1, device_id=peer, device_id_type=MESH)
-
     def vouch(turn):
         for axis in range(2):
             if turn < reach[axis]:
@@ -111,7 +108,11 @@
         load(left_dims_hbm, left_dims, 5),
         load(right_dims_hbm, right_dims, 6),
     ]
-    for copy in loads:
+    for copy in loads[:2]:
+        copy.start()
+    for peer in greeted:
+        pl.semaphore_signal(barrier, inc=1, device_id=peer, device_id_type=MESH)
+    for copy in loads[2:]:
         copy.start()
 
     row_h = lax.broadcasted_iota(jnp.int32, (half, half), 0)
@@ -141,8 +142,8 @@
 
     def ops_copies(t):
         return (
-            send(pack_l.at[t], got_l.at[t], pack_send.at[0, t], pack_recv.at[0, t], down, lane),
-            send(pack_r.at[t], got_r.at[t], pack_send.at[1, t], pack_recv.at[1, t], up, lane),
+            send(pack_l.at[t], got_l.at[t], pack_send.at[0], pack_recv.at[0, t], down, lane),
+            send(pack_r.at[t], got_r.at[t], pack_send.at[1], pack_recv.at[1, t], up, lane),
         )
 
     def prepare_both(t):
@@ -154,45 +155,55 @@
     def start(*copies):
         for copy in copies:
             copy.start()
+
+    def start_one(*copies):
+        start(*copies)
         waits.extend(copies)
 
     def rows(ref, first, count):
         return ref.at[..., pl.ds(pl.multiple_of(first, count), count), :]
+
+    def top(ref, count):
+        return ref.at[..., pl.ds(0, count), :]
 
     def gather_start(ref, slot):
         hr, qr = ref.shape[-2] // 2, ref.shape[-2] // 2 // xs
         own = rows(ref, c * hr + x * qr, qr)
-        for i, d in enumerate(far_first):
-            start(send(own, own, x_send.at[slot, i], x_recv.at[slot, x], me, order[i] * CORES + c))
-        start(send(own, own, c_send.at[slot, x], c_recv.at[slot, x], me, partner))
+        for i in range(xs - 1):
+            start(send(own, own, all_x.at[slot], all_x_in.at[slot, x], me, order[i] * CORES + c))
+        start(send(own, own, all_core.at[slot], all_core_in.at[slot], me, partner))
+        most = top(ref, (xs - 1) * qr)
+        waits.append(send(most, most, all_x.at[slot], all_x_in.at[slot, x], me, order[0] * CORES + c))
+        most = top(ref, hr)
+        waits.append(send(most, most, all_core.at[slot], all_core_in.at[slot], me, partner))
 
     def gather_pass(ref, slot):
         hr, qr = ref.shape[-2] // 2, ref.shape[-2] // 2 // xs
-        for i in reversed(range(len(far_first))):
+        for i in reversed(range(xs - 1)):
             piece = rows(ref, c * hr + order[i] * qr, qr)
             send(
-                piece, piece, x_send.at[slot, i], x_recv.at[slot, order[i]], me, order[i] * CORES + c
+                piece, piece, all_x.at[slot], all_x_in.at[slot, order[i]], me, order[i] * CORES + c
             ).wait_recv()
-            start(send(piece, piece, c_send.at[slot, order[i]], c_recv.at[slot, order[i]], me, partner))
+            start(send(piece, piece, all_core.at[slot], all_core_in.at[slot], me, partner))
 
     def gather_end(ref, slot):
-        hr, qr = ref.shape[-2] // 2, ref.shape[-2] // 2 // xs
-        for i in range(xs):
-            piece = rows(ref, (1 - c) * hr + i * qr, qr)
-            send(piece, piece, c_send.at[slot, i], c_recv.at[slot, i], me, partner).wait_recv()
+        hr = ref.shape[-2] // 2
+        piece = rows(ref, (1 - c) * hr, hr)
+        send(piece, piece, all_core.at[slot], all_core_in.at[slot], me, partner).wait_recv()
 
     def core_copies(buf, core, slot):
         hr, qr = core.shape[-2], core.shape[-2] // xs
         return [
             send(
                 rows(buf, (1 - c) * hr + xi * qr, qr), rows(core, xi * qr, qr),
-                c_send.at[slot, i], c_recv.at[slot, i], me, partner,
+                sum_core.at[slot], sum_core_in.at[slot, i], me, partner,
             )
             for i, xi in enumerate(order)
         ]
 
     def scatter_start(buf, core, slot):
         start(*core_copies(buf, core, slot))
+        waits.append(send(core, core, sum_core.at[slot], sum_core_in.at[slot, 0], me, partner))
 
     def scatter_pass(buf, core, halved, part, slot):
         hr, qr = core.shape[-2], core.shape[-2] // xs
@@ -204,38 +215,40 @@
             if i < xs - 1:
                 piece = rows(halved, xi * qr, qr)
                 piece[...] = mine
-                now = send(
-                    piece, part.at[x], x_send.at[slot, i], x_recv.at[slot, x], me, xi * CORES + c
-                )
+                now = send(piece, part.at[x], sum_x.at[slot], sum_x_in.at[slot], me, xi * CORES + c)
             else:
                 part[x] = mine
                 now = None
             if late is not None:
                 start(late)
             late = now
-
-    def scatter_end(halved, part, slot):
-        qr = halved.shape[-2] // xs
-        for i in range(xs - 1):
-            send(
-                rows(halved, order[i] * qr, qr), part.at[order[i]],
-                x_send.at[slot, i], x_recv.at[slot, order[i]], me, order[i] * CORES + c,
-            ).wait_recv()
+        most = top(halved, (xs - 1) * qr)
+        waits.append(send(most, most, sum_x.at[slot], sum_x_in.at[slot], me, order[0] * CORES + c))
+
+    def scatter_end(part, slot):
+        most = part.at[pl.ds(0, xs - 1)]
+        send(most, most, sum_x.at[slot], sum_x_in.at[slot], me, order[0] * CORES + c).wait_recv()
         total = part[0]
         for i in range(1, xs):
             total = total + part[i]
         return total
 
+    def scalar_all(rnd, stage):
+        count = len(groups[stage])
+        most = sums.at[rnd, stage, pl.ds(0, count)]
+        index = rnd if rnd < 2 else 2 + stage
+        return send(most, most, s_send.at[index], s_recv.at[index], *groups[stage][0][0])
+
     def scalar_start(rnd, stage, value):
         sums[rnd, stage, places[stage]] = value
         own = sums.at[rnd, stage, places[stage]]
-        for d, (peer, _) in enumerate(groups[stage]):
-            start(send(own, own, s_send.at[rnd, stage, d], s_recv.at[rnd, stage, places[stage]], *peer))
+        index = rnd if rnd < 2 else 2 + stage
+        for peer, _ in groups[stage]:
+            start(send(own, own, s_send.at[index], s_recv.at[index], *peer))
+        waits.append(scalar_all(rnd, stage))
 
     def scalar_wait(rnd, stage):
-        for d, (peer, place) in enumerate(groups[stage]):
-            slot = sums.at[rnd, stage, place]
-            send(slot, slot, s_send.at[rnd, stage, d], s_recv.at[rnd, stage, place], *peer).wait_recv()
+        scalar_all(rnd, stage).wait_recv()
         total = sums[rnd, stage, 0]
         for i in range(1, len(groups[stage]) + 1):
             total = total + sums[rnd, stage, i]
@@ -263,7 +276,7 @@
         rows(psi.at[2], c * half + x * psi_rows, psi_rows), psi_piece,
         one_send.at[0], one_recv.at[0], up, lane,
     )
-    start(psi_copy)
+    start_one(psi_copy)
     for copy in loads[3:]:
         copy.wait()
 
@@ -367,7 +380,7 @@
     acc_b[...] = jnp.zeros_like(acc_b)
     nacc[...] = jnp.zeros_like(nacc)
 
-    @pl.loop(0, terms, unroll=True)
+    @pl.loop(0, terms, unroll=4)
     def _(t):
         part_own(t, vec, img_a, acc)
 
@@ -375,10 +388,10 @@
     h_zero, a_zero = norms(0)
     scalar_start(0, 0, row_of([h_zero, a_zero]))
     psi_copy.wait_recv()
-    gather_start(got_psi, 8)
+    gather_start(got_psi, 0)
     scatter_pass(acc_of[0], core_of[0], half_of[0], part_of[0], 0)
 
-    @pl.loop(0, terms, unroll=True)
+    @pl.loop(0, terms, unroll=4)
     def _(t):
         grow(0, 0, img_a, img_a, t)
 
@@ -388,12 +401,12 @@
         part_one(t, vec, img_a, acc)
     vouched(0)
     vouch(1)
-    gather_pass(got_psi, 8)
+    gather_pass(got_psi, 0)
     level_zero = level_of(0)
-    shard = scatter_end(half_of[0], part_of[0], 0)
+    shard = scatter_end(part_of[0], 0)
     correct(0, level_zero, shard)
-    gather_start(cor_of[0], 9)
-    gather_end(got_psi, 8)
+    gather_start(cor_of[0], 1)
+    gather_end(got_psi, 0)
     vec[2] = jnp.where(mask_of(2, 0, width), got_psi[...].astype(F32), 0.0).astype(BF16)
     for t in range(early):
         part_two(t, vec, img_a, acc)
@@ -404,14 +417,14 @@
         part_two(t, vec, img_a, acc)
     vouched(1)
     vouch(2)
-    gather_pass(cor_of[0], 9)
+    gather_pass(cor_of[0], 1)
     for t in range(middle, middle + 1):
         arrive(t)
         part_one(t, vec, img_a, acc)
         part_two(t, vec, img_a, acc)
-    gather_end(cor_of[0], 9)
-
-    @pl.loop(0, terms, unroll=True)
+    gather_end(cor_of[0], 1)
+
+    @pl.loop(0, terms, unroll=4)
     def _(t):
         part_own(t, cor, img_b, acc_b)
 
@@ -427,14 +440,14 @@
     h_near, a_near = norms(1)
     scalar_start(1, 0, row_of([h_near, a_near]))
 
-    @pl.loop(0, terms, unroll=True)
+    @pl.loop(0, terms, unroll=4)
     def _(t):
         grow(1, 0, img_b, img_b, t)
 
     scatter_pass(acc_of[1], core_of[1], half_of[1], part_of[1], 1)
     scatter_pass(acc_of[2], core_of[2], half_of[2], part_of[2], 6)
 
-    @pl.loop(0, terms, unroll=True)
+    @pl.loop(0, terms, unroll=4)
     def _(t):
         grow(2, 0, img_a, img_b, t)
 
@@ -443,37 +456,37 @@
     put_cross(2, 0, vec, cor)
     scatter_start(mats.at[0], core_m.at[0], 2)
     level_near = level_of(1)
-    shard = scatter_end(half_of[1], part_of[1], 1)
+    shard = scatter_end(part_of[1], 1)
     correct(1, level_near, shard)
-    gather_start(cor_of[1], 10)
-    shard = scatter_end(half_of[2], part_of[2], 6)
+    gather_start(cor_of[1], 2)
+    shard = scatter_end(part_of[2], 6)
     correct(2, level_near, shard)
-    gather_start(cor_of[2], 7)
-
-    @pl.loop(0, terms, unroll=True)
+    gather_start(cor_of[2], 3)
+
+    @pl.loop(0, terms, unroll=4)
     def _(t):
         grow(0, 1, img_a, img_a, t)
 
     put_plain(0, 1, vec)
     scatter_start(mats.at[1, 0], core_m.at[1, 0], 3)
-    gather_pass(cor_of[1], 10)
-    gather_end(cor_of[1], 10)
-
-    @pl.loop(0, terms, unroll=True)
+    gather_pass(cor_of[1], 2)
+    gather_end(cor_of[1], 2)
+
+    @pl.loop(0, middle, unroll=True)
     def _(t):
         part_one(t, cor, img_b, acc_b)
 
-    gather_pass(cor_of[2], 7)
-
-    @pl.loop(0, terms, unroll=True)
-    def _(t):
-        nacc[1, 1] += dot_t(img_b[t, 1], img_b[t, 1])
-
-    gather_end(cor_of[2], 7)
+    gather_pass(cor_of[2], 3)
+
+    @pl.loop(middle, terms, unroll=True)
+    def _(t):
+        part_one(t, cor, img_b, acc_b)
+
+    gather_end(cor_of[2], 3)
     tag_out[...] = jnp.broadcast_to(level_near, (8, half))
     scatter_pass(mats.at[0], core_m.at[0], half_m.at[0], part_m, 2)
 
-    @pl.loop(0, terms, unroll=True)
+    @pl.loop(0, terms, unroll=4)
     def _(t):
         part_two(t, cor, img_b, acc_b)
 
@@ -502,14 +515,14 @@
     scalar_start(2, 1, row_of(gathered))
     scatter_pass(mats.at[1, 0], core_m.at[1, 0], half_m.at[1, 0], part_n.at[0], 3)
 
-    @pl.loop(0, terms, unroll=True)
-    def _(t):
-        nacc[1, 1] += dot_t(img_b[t, 2], img_b[t, 2])
+    @pl.loop(0, terms, unroll=4)
+    def _(t):
+        grow(1, 1, img_b, img_b, t)
 
     put_plain(1, 1, cor)
     scatter_start(mats.at[1, 1], core_m.at[1, 1], 4)
 
-    @pl.loop(0, terms, unroll=True)
+    @pl.loop(0, terms, unroll=4)
     def _(t):
         grow(2, 1, img_a, img_b, t)
 
@@ -521,16 +534,16 @@
         send(cor.at[2], cor_got, one_send.at[2], one_recv.at[2], down, lane),
         send(tag_out, tag_in, one_send.at[3], one_recv.at[3], down, lane),
     ]
-    start(*to_owner)
+    start_one(*to_owner)
     scatter_pass(mats.at[1, 2], core_m.at[1, 2], half_m.at[1, 2], part_n.at[2], 5)
     scalar_start(2, 0, scalar_wait(2, 2))
-    stay = scatter_end(half_m.at[0], part_m, 2)
+    stay = scatter_end(part_m, 2)
     count = stay.shape[1]
     for q in range(3):
-        hop_out[q * count:(q + 1) * count] = scatter_end(half_m.at[1, q], part_n.at[q], 3 + q)
+        hop_out[q * count:(q + 1) * count] = scatter_end(part_n.at[q], 3 + q)
     hop_out[3 * count:] = jnp.broadcast_to(level_near, (8, half))
     hop = send(hop_out, hop_in, one_send.at[1], one_recv.at[1], up, lane)
-    start(hop)
+    start_one(hop)
     whole = column_of(scalar_wait(2, 0))
     a11, h11, v_u, u_u, v_hu, u_hu = [whole[q:q + 1] for q in range(6)]
     mean = h11 / a11
@@ -558,7 +571,7 @@
     come = weigh(coef_last, [hop_in[q * count:(q + 1) * count] for q in range(3)])
     piled = folded.at[pl.ds(0, 3 * half)]
     rows(piled, (c * xs + x) * count, count)[...] = stay + come
-    gather_start(piled, 11)
+    gather_start(piled, 4)
     for copy in to_owner:
         copy.wait_recv()
     coefs.append(first_coef + second_coef * (tag_in[0:1, 0:1] - mean))
@@ -574,15 +587,12 @@
     folded[3 * half:] = jnp.where(tail == 0, live, lowest)
     state_copy = load(ns_mine, state_hbm, 7)
     state_copy.start()
-    gather_pass(piled, 11)
-    gather_end(piled, 11)
+    gather_pass(piled, 4)
+    gather_end(piled, 4)
     folded_copy = load(folded, folded_hbm, 8)
     folded_copy.start()
-    @pl.loop(0, terms)
-    def _(t):
-        for copy in ops_copies(t):
-            copy.wait_send()
-
+    send(pack_l, got_l, pack_send.at[0], pack_recv.at[0, 0], down, lane).wait_send()
+    send(pack_r, got_r, pack_send.at[1], pack_recv.at[1, 0], up, lane).wait_send()
     for copy in waits:
         copy.wait_send()
     state_copy.wait()
@@ -613,10 +623,13 @@
 
     def step():
         current = kept[...]
-        parts = halves(current)
-        squared = dot_wide(parts, parts)
-        cubed = dot_wide(halves(squared), parts)
-        kept[...] = 1.5 * current - 0.5 * cubed
+        high, low = halves(current)
+        stacked = jnp.concatenate([high, low, high], axis=0)
+        for first in range(0, width, half):
+            block = slice(first, first + half)
+            squared = dot(beside(high[block], low[block]), stacked)
+            cubed = dot(beside(*halves(squared)), stacked)
+            kept[block] = 1.5 * current[block] - 0.5 * cubed
 
     pl.loop(0, SIGN_STEPS // 2)(lambda _: step())
     into.wait()
@@ -663,10 +676,10 @@
         + [pltpu.VMEM((3, 3, most, 1, half), F32)]
         + [pltpu.VMEM((3, width, width), BF16), pltpu.VMEM((width, width), BF16)]
         + [pltpu.VMEM((8, half), F32)] * 2
-        + [dma((9,)), dma((2, terms)), dma((2, terms)), dma((4,)), dma((4,))]
-        + [dma((12, xs))] * 4
-        + [dma((3, 3, most))] * 2
-        + [pltpu.SemaphoreType.REGULAR((2, max(zs // 2, ys // 2), 2))],
+        + [dma((9,)), dma((2,)), dma((2, terms)), dma((4,)), dma((4,))]
+        + [dma((7,)), dma((7, xs)), dma((7,)), dma((7,)), dma((5,)), dma((5,)), dma((5,)), dma((5, xs))]
+        + [dma((5,))] * 2
+        + [pltpu.SemaphoreType.REGULAR((2, max(zs // 2, ys // 2, 2) - 1, 2))],
         compiler_params=pltpu.CompilerParams(
             collective_id=0, has_side_effects=True, vmem_limit_bytes=67043328
         ),

time: 72.1 us -> 68.6 us (0.951)
  Pallas kernels: 71.3 us -> 67.8 us
    pallas_call x1, Pallas kernels: 65.6 us -> 62.5 us  [per_device(): pl.pallas_call(functools.partial(kernel, (ns, zs, tg, terms, width)), out...]
where the time goes in v6:
time: 68.6 us; the launch traced here: 68.4 us
  Pallas kernels  67.8 us (99%)
    pallas_call x1, Pallas kernels, per_device(): pl.pallas_call(functools.partial(kernel, (ns, zs, tg, terms, width)), out...  62.5 us
    pallas_call x1, Pallas kernels, per_device(): pl.pallas_call(functools.partial(sign_kernel, half), out_shape=(jax.Shape...  5.32 us

profile of v6, /device:TPU:1, one launch (start us, length us, event | category | flops | bytes accessed | tf_op | source)
XLA Modules:
  0.0 68.4 jit_solution(12682146583897690726)
XLA Ops:
  0.6 62.5 %shard_map.76 = (bf16[3,256,256]{2,1,0:T(8,128)(2,1)}, f32[392,128]{1,0:T(8,128)}) custom-call(s32[64]{0:T(128)} %left_dims_hbm.1, s32[64]{0:T(128)} %right_dims_hbm.1, bf16[3,256,256]{2,1,0:T(8,128)(2,1)} %bitcast.8, bf16[8,256,256]{2,1,0:T(8,128)(2,1)} %bitcast.6, bf16[8,256,256]{2,1,0:T(8,128)(2,1)} %bitcast.7), custom_call_target="tpu_custom_call" | custom-call | tf_op jit(solution)/shard_map/pallas_call | solution.py:651
  63.1 5.3 %shard_map.77 = (bf16[3,256,256]{2,1,0:T(8,128)(2,1)}, f32[256,256]{1,0:T(8,128)}, f32[1,1]{1,0:T(1,128)}) custom-call(f32[392,128]{1,0:T(8,128)} %get-tuple-element.8.folded, bf16[3,256,256]{2,1,0:T(8,128)(2,1)} %get-tuple-element.9.state_hbm), custom_call_target="tpu_custom_call" | custom-call | tf_op jit(solution)/shard_map/pallas_call | solution.py:687

commit v7 on v6

--- a/solution.py
+++ b/solution.py
@@ -380,7 +380,7 @@
     acc_b[...] = jnp.zeros_like(acc_b)
     nacc[...] = jnp.zeros_like(nacc)
 
-    @pl.loop(0, terms, unroll=4)
+    @pl.loop(0, terms, unroll=True)
     def _(t):
         part_own(t, vec, img_a, acc)
 
@@ -482,27 +482,32 @@
     def _(t):
         part_one(t, cor, img_b, acc_b)
 
+
+    def overlaps(k):
+        wide, corr = vec[k].astype(F32), cor[k].astype(F32)
+        return fold(wide * corr), fold(corr * corr)
+
+    plain = [overlaps(0), overlaps(1)]
     gather_end(cor_of[2], 3)
     tag_out[...] = jnp.broadcast_to(level_near, (8, half))
     scatter_pass(mats.at[0], core_m.at[0], half_m.at[0], part_m, 2)
 
-    @pl.loop(0, terms, unroll=4)
+    @pl.loop(0, terms, unroll=True)
     def _(t):
         part_two(t, cor, img_b, acc_b)
 
+    plain[1] = [one + two for one, two in zip(plain[1], overlaps(2))]
     levels = [level_zero, level_near]
     sides = [(h_zero, a_zero), (h_near, a_near)]
     gathered = [jnp.zeros((1, half), F32)] * 6
     for team in range(2):
         level, (h_row, a_row) = levels[team], sides[team]
-        vc = cc = vhc = chc = jnp.zeros((1, half), F32)
+        vc, cc = plain[team]
+        vhc = chc = jnp.zeros((1, half), F32)
         for k in teams[team]:
-            wide, corr = vec[k].astype(F32), cor[k].astype(F32)
             summed = acc_b[k]
-            vc = vc + fold(wide * corr)
-            cc = cc + fold(corr * corr)
-            vhc = vhc + fold(wide * summed)
-            chc = chc + fold(corr * summed)
+            vhc = vhc + fold(vec[k].astype(F32) * summed)
+            chc = chc + fold(cor[k].astype(F32) * summed)
         here = [
             a_row * each,
             h_row,
@@ -515,7 +520,7 @@
     scalar_start(2, 1, row_of(gathered))
     scatter_pass(mats.at[1, 0], core_m.at[1, 0], half_m.at[1, 0], part_n.at[0], 3)
 
-    @pl.loop(0, terms, unroll=4)
+    @pl.loop(0, terms, unroll=True)
     def _(t):
         grow(1, 1, img_b, img_b, t)
 

time: 68.6 us -> 68.9 us (level)
  no operation moved by 1% of the time
where the time goes in v7:
time: 68.9 us; the launch traced here: 68.7 us
  Pallas kernels  68.1 us (99%)
    pallas_call x1, Pallas kernels, per_device(): pl.pallas_call(functools.partial(kernel, (ns, zs, tg, terms, width)), out...  62.8 us
    pallas_call x1, Pallas kernels, per_device(): pl.pallas_call(functools.partial(sign_kernel, half), out_shape=(jax.Shape...  5.32 us

profile of v7, /device:TPU:1, one launch (start us, length us, event | category | flops | bytes accessed | tf_op | source)
XLA Modules:
  0.0 68.7 jit_solution(8925657245846278827)
XLA Ops:
  0.6 62.8 %shard_map.76 = (bf16[3,256,256]{2,1,0:T(8,128)(2,1)}, f32[392,128]{1,0:T(8,128)}) custom-call(s32[64]{0:T(128)} %left_dims_hbm.1, s32[64]{0:T(128)} %right_dims_hbm.1, bf16[3,256,256]{2,1,0:T(8,128)(2,1)} %bitcast.8, bf16[8,256,256]{2,1,0:T(8,128)(2,1)} %bitcast.6, bf16[8,256,256]{2,1,0:T(8,128)(2,1)} %bitcast.7), custom_call_target="tpu_custom_call" | custom-call | tf_op jit(solution)/shard_map/pallas_call | solution.py:656
  63.4 5.3 %shard_map.77 = (bf16[3,256,256]{2,1,0:T(8,128)(2,1)}, f32[256,256]{1,0:T(8,128)}, f32[1,1]{1,0:T(1,128)}) custom-call(f32[392,128]{1,0:T(8,128)} %get-tuple-element.8.folded, bf16[3,256,256]{2,1,0:T(8,128)(2,1)} %get-tuple-element.9.state_hbm), custom_call_target="tpu_custom_call" | custom-call | tf_op jit(solution)/shard_map/pallas_call | solution.py:692
